TPU v7x, 128 devices: a whole 4x4x4 slice. The times are simulated.
128 devices in a mesh: ens: 4 (over z_lo, core), grid: 32 (over z_hi, y, x).
Axes of the slice: x: 4, y: 4, z: 4 (z_hi: 2, z_lo: 2; z = z_hi * 2 + z_lo), core: 2. Of those that a mesh axis runs over, the one named last changes fastest.
Arguments:
- encoded_state: bfloat16 [8, 1024, 32768], P('ens', None, 'grid'), may hold values from -6 to 6
- observed_state: float32 [80, 32768], P(None, 'grid'), may hold values from -6 to 6
- location_importance: float32 [32768], P('grid'), may hold values from 0.5 to 5
- w_in: bfloat16 [1024, 1024], replicated, may hold values from -0.1875 to 0.1875
- b_in: float32 [1024], replicated, may hold values from -3 to 3
- final_matrix: bfloat16 [80, 1024], replicated, may hold values from -0.1875 to 0.1875
Outputs:
- latent_sensitivity: bfloat16 [8, 1024, 32768], P('ens', None, 'grid')
- grad_w_in: float32 [1024, 1024], P('grid')
- grad_w_out: float32 [80, 1024], replicated
- grad_b_in: float32 [1024], replicated
All inputs are finite; a program needn't handle non-finite values.
Results may differ from a plain program's by a relative error of at most 0.0025.
The roundings to bfloat16 on the way count: a program that leaves them out, or rounds other values in their place, can miss the bound.
Values sent between devices are 32-bit elements; how exact they have to be, the bound alone decides.
No kernel may reach another device: no remote copies, remote signals or barrier semaphores. Data moves between devices by JAX's collectives and lax.ppermute only.
A program may use at most 128 MiB of HBM per device.

v0:
```python
import functools
import math

import jax
import jax.numpy as jnp
from jax import lax
from jax.experimental import pallas as pl
from jax.experimental.pallas import tpu as pltpu
from jax.sharding import PartitionSpec as P


delta_abs = 0.1
fair_alpha = 0.95
AXES = ("ens", "grid")
F32, BF16 = jnp.float32, jnp.bfloat16
HALVES = 2
ROOT = math.sqrt(2.0 / math.pi)
CUBIC = 0.044715
CHUNK = 512
FIRST, LATER = 48, 36


def decode(index):
    e, g = divmod(index, 32)
    zl, c = divmod(e, 2)
    zh, r = divmod(g, 16)
    y, x = divmod(r, 4)
    return x, y, zh * 2 + zl, c


def encode(x, y, z, c):
    return ((z % 2) * 2 + c) * 32 + (z // 2) * 16 + y * 4 + x


SWAP_CORE = [(i, encode(*decode(i)[:3], 1 - decode(i)[3])) for i in range(128)]
SWAP_Z = [(i, encode(decode(i)[0], decode(i)[1], decode(i)[2] ^ 1, decode(i)[3])) for i in range(128)]
HIGH = ((0, 1, 1, 0), (0, 0, 1, 1))
LOW = ((0, 0, 1, 1), (0, 1, 1, 0))


def cubes(stage):
    found = {}
    for index in range(128):
        x, y, z, c = decode(index)
        digits, others = (HIGH, LOW) if stage == 0 else (LOW, HIGH)
        place = (digits[c][x], digits[c][y], digits[1 - c][z])
        rest = (others[c][x], others[c][y], others[1 - c][z])
        found.setdefault((c, rest), []).append((place, index))
    return [[index for _, index in sorted(v)] for _, v in sorted(found.items())]


CUBES = (cubes(0), cubes(1))


def block_order(c):
    coordinate = {(HIGH[c][u], LOW[c][u]): u for u in range(4)}
    order = []
    for place in range(64):
        kx1, ky1, kz1, kx2, ky2, last = ((place >> s) & 1 for s in (5, 4, 3, 2, 1, 0))
        x, y = coordinate[kx1, kx2], coordinate[ky1, ky2]
        zh, half = (last, kz1) if c == 1 else (kz1, last)
        order.append(((zh * 4 + y) * 4 + x) * 2 + half)
    return order


ORDER = (block_order(0), block_order(1))


def all_to_all(value, groups):
    return lax.all_to_all(value, AXES, 0, 0, axis_index_groups=groups, tiled=True)


def dot(a, b):
    return jnp.dot(a, b, preferred_element_type=F32)


def dot_nt(a, b):
    return lax.dot_general(a, b, (((1,), (1,)), ((), ())), preferred_element_type=F32)


def dot_tn(a, b):
    return lax.dot_general(a, b, (((0,), (0,)), ((), ())), preferred_element_type=F32)


def params(mib=60):
    return pltpu.CompilerParams(vmem_limit_bytes=mib << 20)


def cost(flops, bytes_accessed):
    return pl.CostEstimate(flops=flops, bytes_accessed=bytes_accessed, transcendentals=0)


def forward_rows(i, r, x, w_ref, column_ref, f_ref, hidden_ref, slope_ref):
    rows = pl.ds(r, CHUNK)
    v = dot(w_ref[rows, :], x) + column_ref[rows, :]
    v2 = v * v
    t = jnp.tanh(v * (ROOT * CUBIC * v2 + ROOT))
    a = 0.5 * t + 0.5
    hidden = (v * a).astype(BF16)
    hidden_ref[i, rows, :] = hidden
    slope_ref[i, rows, :] = a + (v * (1.5 * ROOT * CUBIC * v2 + 0.5 * ROOT)) * (1.0 - t * t)
    return dot(f_ref[:, rows], hidden)


def forward_kernel(half, first, x_any, w_any, b_any, f_any, hidden_ref, slope_ref, fc_ref, *refs):
    m, h, n = hidden_ref.shape
    starts = range(0, h, CHUNK)
    if first:
        w_ref, column_ref, x_ref, b_ref, f_ref, sems = refs
    else:
        w_ref, column_ref, f_ref, (x_ref, sems) = w_any, b_any, f_any, refs

    def copy(source, target, k):
        return pltpu.make_async_copy(source, target, sems.at[k])

    fetch_x = [copy(x_any.at[i, :, pl.ds(half * n, n)], x_ref.at[i], i) for i in range(m)]
    if first:
        fetch_b, fetch_f = copy(b_any, b_ref, m), copy(f_any, f_ref, m + 1)
        fetch_w = [copy(w_any.at[pl.ds(r, CHUNK)], w_ref.at[pl.ds(r, CHUNK)], m + 2 + j) for j, r in enumerate(starts)]
        for one in [fetch_b] + fetch_w[:1] + fetch_x[:1] + [fetch_f] + fetch_w[1:] + fetch_x[1:]:
            one.start()
        fetch_b.wait()
        turned = b_ref[...].T
        for i in range(turned.shape[1]):
            column_ref[128 * i : 128 * i + 128, :] = turned[:, i : i + 1]
    else:
        for one in fetch_x:
            one.start()
    for i in range(m):
        total = None
        fetch_x[i].wait()
        for j, r in enumerate(starts):
            if first and i == 0:
                fetch_w[j].wait()
                if j == 0:
                    fetch_f.wait()
            part = forward_rows(i, r, x_ref[i], w_ref, column_ref, f_ref, hidden_ref, slope_ref)
            total = part if total is None else total + part
        fc_ref[i] = total


VMEM = pl.BlockSpec(memory_space=pltpu.VMEM)
HBM = pl.BlockSpec(memory_space=pltpu.HBM)


def forward(state, w_in, bias, final_matrix, half, first):
    m, d, g = state.shape
    h, c = w_in.shape[0], final_matrix.shape[0]
    n = g // HALVES
    results = [
        jax.ShapeDtypeStruct((m, h, n), BF16),
        jax.ShapeDtypeStruct((m, h, n), F32),
        jax.ShapeDtypeStruct((m, c, n), F32),
    ]
    scratch = [pltpu.VMEM((m, d, n), BF16)]
    if first:
        results += [jax.ShapeDtypeStruct((h, d), BF16), jax.ShapeDtypeStruct((h, 1), F32)]
        scratch += [pltpu.VMEM(bias.shape, F32), pltpu.VMEM((c, h), BF16)]
    return pl.pallas_call(
        functools.partial(forward_kernel, half, first),
        in_specs=[HBM] * 4 if first else [HBM] + [VMEM] * 3,
        out_specs=[VMEM] * len(results),
        out_shape=results,
        scratch_shapes=scratch + [pltpu.SemaphoreType.DMA((m + 2 + h // CHUNK,))],
        compiler_params=params(FIRST if first else LATER),
        cost_estimate=cost(2 * m * h * n * (d + c), m * n * (2 * d + 6 * h)),
    )(state, w_in, bias, final_matrix)


def slope_of(d):
    return d * lax.rsqrt(d * d + delta_abs * delta_abs)


def backward_kernel(factor, half, own_ref, a_ref, b_ref, c_ref, obs_ref, loc_ref, f_ref, slope_ref, hidden_ref,
                    *refs):
    init, (gp_ref, small_ref, wide_ref, bias_ref) = refs[:-4], refs[-4:]
    m, channels, n = own_ref.shape
    here = slice(half * n, half * n + n)
    ones = jnp.ones((8, n), BF16)
    for i in range(m):
        own = own_ref[i]
        pairs = None
        for ref in (own_ref, a_ref, b_ref, c_ref):
            for k in range(m):
                s = slope_of(own - ref[k])
                pairs = s if pairs is None else pairs + s
        grad = (loc_ref[:, here] * (slope_of(own - obs_ref[:, here]) - factor * pairs)).astype(BF16)
        for r in range(0, f_ref.shape[1], CHUNK):
            rows = pl.ds(r, CHUNK)
            gp = (dot_tn(f_ref[:, rows], grad) * slope_ref[i, rows, :]).astype(BF16)
            gp_ref[i, rows, :] = gp
            wide = dot_nt(hidden_ref[i, rows, :], grad)
            bias = dot_nt(gp, ones)
            if i == 0:
                wide_ref[rows, :channels] = wide
                bias_ref[rows, :] = bias
            else:
                wide_ref[rows, :channels] += wide
                bias_ref[rows, :] += bias
    wide, bias = wide_ref[...].T[:channels, :], bias_ref[...].T
    if init:
        wide += init[0][:channels, :]
        bias += init[0][channels : channels + 8, :]
    small_ref[:channels, :] = wide
    small_ref[channels : channels + 8, :] = bias
    small_ref[channels + 8 :, :] = jnp.zeros_like(small_ref[channels + 8 :, :])


def backward(fcs, observed, location, final_matrix, slope, hidden, init, factor, half):
    m, h, n = hidden.shape
    operands = (*fcs, observed, location, final_matrix, slope, hidden, *init)
    return pl.pallas_call(
        functools.partial(backward_kernel, factor, half),
        in_specs=[VMEM] * len(operands),
        out_specs=[VMEM, VMEM],
        out_shape=[jax.ShapeDtypeStruct((m, h, n), BF16), jax.ShapeDtypeStruct((128, h), F32)],
        scratch_shapes=[
            pltpu.VMEM((h, 128), F32),
            pltpu.VMEM((h, 8), F32),
        ],
        compiler_params=params(16),
        cost_estimate=cost(4 * m * h * n * 256, m * n * 8 * h),
    )(*operands)


def weight_kernel(other, *refs):
    gps, (x_ref, *rest) = refs[:HALVES], refs[HALVES:]
    out_ref = rest[-1]
    m, h, n = gps[0].shape
    columns = out_ref.shape[1]
    core = lax.rem(lax.axis_index("ens"), 2)
    own = pl.ds(pl.multiple_of((1 - core if other else core) * columns, columns), columns)
    for r in range(0, h, CHUNK):
        rows = pl.ds(r, CHUNK)
        out_ref[rows, :] = sum(
            dot_nt(gp[i, rows, :], x_ref[i, own, k * n : (k + 1) * n]) for i in range(m) for k, gp in enumerate(gps)
        )
    if other:
        out_ref[h:, :] = rest[0][:, own]


def weight_half(gps, state, *small):
    m, d, g = state.shape
    h = gps[0].shape[1]
    rows = h + sum(one.shape[0] for one in small)
    return pl.pallas_call(
        functools.partial(weight_kernel, bool(small)),
        in_specs=[VMEM] * (HALVES + 1 + len(small)),
        out_specs=VMEM,
        out_shape=jax.ShapeDtypeStruct((rows, d // 2), F32),
        compiler_params=params(16),
        cost_estimate=cost(m * h * d * g, m * g * (2 * h + d) + 2 * h * d),
        name="theirs" if small else "mine",
    )(*gps, state, *small)


def blocks_kernel(mine_ref, got_ref, small_ref, out_ref):
    core = lax.rem(lax.axis_index("ens"), 2)
    h, columns = mine_ref.shape
    own = pl.ds(pl.multiple_of(core * columns, columns), columns)

    def fill(order):
        for place, block in enumerate(order):
            k, j = divmod(place, 8)
            rows = slice(16 * block, 16 * block + 16)
            out_ref[k, 16 * j : 16 * j + 16, :] = mine_ref[rows, :] + got_ref[rows, :]

    pl.when(core == 0)(lambda: fill(ORDER[0]))
    pl.when(core != 0)(lambda: fill(ORDER[1]))
    for k in range(8):
        rows = slice(16 * k, 16 * k + 16)
        out_ref[k, 128:, :] = small_ref[rows, own] + got_ref[h + 16 * k : h + 16 * k + 16, :]


def make_blocks(mine, got, small):
    return pl.pallas_call(
        blocks_kernel,
        in_specs=[VMEM] * 3,
        out_specs=VMEM,
        out_shape=jax.ShapeDtypeStruct((8, 144, 512), F32),
        compiler_params=params(16),
        cost_estimate=cost(1 << 19, 7 << 20),
        name="blocks",
    )(mine, got, small)


def gather_kernel(second_ref, out_ref, kept_ref):
    total = second_ref[0]
    for k in range(1, second_ref.shape[0]):
        total = total + second_ref[k]
    kept_ref[...] = total[:32]
    for k in range(out_ref.shape[0]):
        out_ref[k, :16, :] = total[32:]
        out_ref[k, 16:, :] = total[:16]


def gather_blocks(second):
    return pl.pallas_call(
        gather_kernel,
        in_specs=[VMEM],
        out_specs=[VMEM] * 2,
        out_shape=[jax.ShapeDtypeStruct((8, 32, 512), F32), jax.ShapeDtypeStruct((32, 512), F32)],
        compiler_params=params(16),
        name="gather",
    )(second)


def pick_kernel(kept_ref, third_ref, out_ref):
    core = lax.rem(lax.axis_index("ens"), 2)
    x = lax.rem(lax.axis_index("grid"), 4)
    y = lax.rem(lax.div(lax.axis_index("grid"), 4), 4)
    place = 2 * (2 * lax.div(x, 2) + lax.div(y, 2))

    @pl.when(core == 0)
    def _():
        out_ref[:32, :] = kept_ref[...]

    @pl.when(core != 0)
    def _():
        out_ref[:16, :] = third_ref[place, 16:, :]
        out_ref[16:32, :] = third_ref[place + 1, 16:, :]

    for k in range(third_ref.shape[0]):
        out_ref[32 + 16 * k : 48 + 16 * k, :] = third_ref[k, :16, :]


def pick(kept, third):
    return pl.pallas_call(
        pick_kernel,
        in_specs=[VMEM] * 2,
        out_specs=VMEM,
        out_shape=jax.ShapeDtypeStruct((160, 512), F32),
        compiler_params=params(16),
        name="pick",
    )(kept, third)


def finish_kernel(scale, done_ref, other_ref, in_ref, out_ref, bias_ref):
    core = lax.rem(lax.axis_index("ens"), 2)
    columns = done_ref.shape[1]
    for which, ref in ((core, done_ref), (1 - core, other_ref)):
        lanes = pl.ds(pl.multiple_of(columns * which, columns), columns)
        in_ref[:, lanes] = ref[:32, :] * scale
        out_ref[:, lanes] = ref[32:112, :] * scale
        bias_ref[:, lanes] = ref[112:113, :] * scale


def finish(scale, *operands):
    return pl.pallas_call(
        functools.partial(finish_kernel, scale),
        in_specs=[VMEM] * len(operands),
        out_specs=[VMEM] * 3,
        out_shape=[jax.ShapeDtypeStruct(shape, F32) for shape in ((32, 1024), (80, 1024), (1, 1024))],
        compiler_params=params(16),
        name="finish",
    )(*operands)


def latent_kernel(w_ref, *refs):
    gps, out_ref = refs[:HALVES], refs[HALVES]
    n = gps[0].shape[2]
    for k, gp in enumerate(gps):
        out_ref[0, :, k * n : (k + 1) * n] = dot(w_ref[...], gp[0]).astype(BF16)


def latent(wt, gps):
    m, h, n = gps[0].shape
    d = wt.shape[0]
    return pl.pallas_call(
        latent_kernel,
        grid=(m, d // CHUNK),
        in_specs=[pl.BlockSpec((CHUNK, h), lambda i, j: (j, 0))]
        + [pl.BlockSpec((1, h, n), lambda i, j: (i, 0, 0))] * HALVES,
        out_specs=pl.BlockSpec((1, CHUNK, HALVES * n), lambda i, j: (i, j, 0)),
        out_shape=jax.ShapeDtypeStruct((m, d, HALVES * n), BF16),
        compiler_params=params(),
        cost_estimate=cost(2 * m * h * d * n * HALVES, 2 * m * n * HALVES * (h + d)),
        name="latent",
    )(wt, *gps)


def shards(encoded_state, observed_state, location_importance, w_in, b_in, final_matrix):
    members = encoded_state.shape[0] * lax.axis_size("ens")
    points = encoded_state.shape[2] * lax.axis_size("grid")
    bias = b_in.reshape(-1, 128)
    location = location_importance.reshape(1, -1)
    factor = (1.0 - (1.0 - fair_alpha) / members) / (members - 1)

    hiddens, slopes, fcs = [], [], []
    weight = w_in
    for half in range(HALVES):
        hidden, slope, fc, *kept = forward(encoded_state, weight, bias, final_matrix, half, half == 0)
        if kept:
            weight, bias = kept
        hiddens.append(hidden)
        slopes.append(slope)
        across = lax.ppermute(fc, AXES, SWAP_Z)
        fcs.append((fc, across, lax.ppermute(fc, AXES, SWAP_CORE)))
    gps, init = [], ()
    for half in range(HALVES):
        fc, across, beside = fcs[half]
        if gps:
            across, gps[-1] = lax.optimization_barrier((across, gps[-1]))
        else:
            across, hiddens[-1] = lax.optimization_barrier((across, hiddens[-1]))
        diagonal = lax.ppermute(across, AXES, SWAP_CORE)
        everyone = (fc, beside, across, diagonal)
        gp, small = backward(
            everyone, observed_state, location, final_matrix, slopes[half], hiddens[half], init, factor, half
        )
        init = (small,)
        gps.append(gp)
    theirs = weight_half(gps, encoded_state, small)
    got = lax.ppermute(theirs, AXES, SWAP_CORE)
    blocks = make_blocks(weight_half(gps, encoded_state), got, small)
    blocks, late_weight = lax.optimization_barrier((blocks, w_in))
    first = all_to_all(blocks, CUBES[0])
    first, latent_sensitivity = lax.optimization_barrier((first, latent(late_weight.T, gps)))

    core = lax.axis_index("ens") % 2
    first = jnp.sum(first, 0)
    rows, small = first[:128], first[128:]
    split = jnp.broadcast_to(rows.reshape(8, 1, 16, 512), (8, 2, 16, 512)).reshape(8, 32, 512)
    whole = jnp.broadcast_to(rows.reshape(4, 1, 32, 512), (4, 2, 32, 512)).reshape(8, 32, 512)
    send = jnp.concatenate(
        [jnp.where(core == 1, split, whole), jnp.broadcast_to(small[None], (8, 16, 512))], 1
    )
    send, kept = gather_blocks(all_to_all(send, CUBES[1]))
    done = pick(kept, all_to_all(send, CUBES[0]))
    other = lax.ppermute(done, AXES, SWAP_CORE)
    in_sum, out_sum, bias_sum = finish(1.0 / math.sqrt(members * points), done, other)
    return latent_sensitivity, in_sum, out_sum, bias_sum.reshape(-1)


def solution(mesh):
    placed = (P("ens", None, "grid"), P(None, "grid"), P("grid"), P(), P(), P())
    return jax.shard_map(
        shards,
        mesh=mesh,
        in_specs=placed,
        out_specs=(P("ens", None, "grid"), P("grid", None), P(), P()),
        check_vma=False,
    )
```

profile of v0, /device:TPU:1, one launch (start us, length us, event | category | flops | bytes accessed | tf_op | source)
XLA Modules:
  0.0 101.3 jit_solution(2434353801441491321)
XLA Ops:
  0.6 0.0 copy-start.5
  0.6 0.9 copy-done.5
  1.5 0.0 copy-start.8
  1.6 0.7 copy-done.8
  2.2 0.0 copy-start
  2.2 0.0 copy-start.6
  2.2 8.3 %shard_map.93 = (bf16[2,1024,512]{2,1,0:T(8,128)(2,1)S(1)}, f32[2,1024,512]{2,1,0:T(8,128)}, f32[2,80,512]{2,1,0:T(8,128)S(1)}, bf16[1024,1024]{1,0:T(8,128)(2,1)S(1)}, f32[1024,1]{1,0:T(8,128)S(1)}) custom-call(bf16[2,1024,1024]{2,1,0:T(8,128)(2,1)} %refs_2_.3, bf16[1024,1024]{1,0:T(8,128)(2,1)} %w_any.1, f32[8,128]{1,0:T(8,128)S(1)} %bitcast.12, ...), custom_call_target="tpu_custom_call" | custom-call | flops 2315255808 | bytes 8388608 | tf_op jit(solution)/shard_map/pallas_call | solution.py:159
  10.6 2.5 %collective-permute-start.2 = (f32[2,80,512]{2,1,0:T(8,128)S(1)}, f32[2,80,512]{2,1,0:T(8,128)S(1)}, u32[]{:S(2)}, u32[]{:S(2)}) collective-permute-start(f32[2,80,512]{2,1,0:T(8,128)S(1)} %get-tuple-element.32.own_ref), channel_id=1, source_target_pairs={{0,64},{1,65},{2,66},{3,67},{4,68},{5,69},{6,70},{7,71},{8,72},{9,... | collective-permute-start | bytes 983048 | tf_op jit(solution)/shard_map/ppermute | solution.py:397
  13.1 1.0 collective-permute-start.1
  14.1 0.0 copy-done
  14.1 0.0 copy-done.6
  14.1 0.0 copy-start.7
  14.1 4.9 %shard_map.94 = (bf16[2,1024,512]{2,1,0:T(8,128)(2,1)S(1)}, f32[2,1024,512]{2,1,0:T(8,128)S(1)}, f32[2,80,512]{2,1,0:T(8,128)S(1)}) custom-call(bf16[2,1024,1024]{2,1,0:T(8,128)(2,1)S(1)} %copy-done, bf16[1024,1024]{1,0:T(8,128)(2,1)S(1)} %get-tuple-element.29.w_any, f32[1024,1]{1,0:T(8,128)S(1)} %get-tuple-element.30.b_any, bf16[80,1024]{1,0:T(8,128)(2,1)S(1)} %copy-done.6), custom_call_target="tpu_custom_call" | custom-call | flops 2315255808 | bytes 8388608 | tf_op jit(solution)/shard_map/pallas_call | solution.py:159
  19.0 1.5 %collective-permute-done.2.b_ref = f32[2,80,512]{2,1,0:T(8,128)S(1)} collective-permute-done((f32[2,80,512]{2,1,0:T(8,128)S(1)}, f32[2,80,512]{2,1,0:T(8,128)S(1)}, u32[]{:S(2)}, u32[]{:S(2)}) %collective-permute-start.2) | collective-permute-done | bytes 327712 | tf_op jit(solution)/shard_map/ppermute | solution.py:397
  20.5 1.3 %collective-permute-start.3 = (f32[2,80,512]{2,1,0:T(8,128)S(1)}, f32[2,80,512]{2,1,0:T(8,128)S(1)}, u32[]{:S(2)}, u32[]{:S(2)}) collective-permute-start(f32[2,80,512]{2,1,0:T(8,128)S(1)} %collective-permute-done.2.b_ref), channel_id=1, source_target_pairs={{0,32},{1,33},{2,34},{3,35},{4,36},{5,37},{6,38},{7,39},{8,40},{9,... | collective-permute-start | bytes 983048 | tf_op jit(solution)/shard_map/ppermute | solution.py:406
  21.8 1.5 %collective-permute-start = (f32[2,80,512]{2,1,0:T(8,128)S(1)}, f32[2,80,512]{2,1,0:T(8,128)S(1)}, u32[]{:S(2)}, u32[]{:S(2)}) collective-permute-start(f32[2,80,512]{2,1,0:T(8,128)S(1)} %get-tuple-element.31.own_ref), channel_id=1, source_target_pairs={{0,64},{1,65},{2,66},{3,67},{4,68},{5,69},{6,70},{7,71},{8,72},{9,... | collective-permute-start | bytes 983048 | tf_op jit(solution)/shard_map/ppermute | solution.py:397
  23.2 0.3 collective-permute-start.4
  23.5 0.0 collective-permute-done.1.a_ref
  23.5 0.0 collective-permute-done.3.c_ref
  23.5 0.0 copy-done.3
  23.5 0.0 copy-done.4
  23.5 0.0 copy-done.7
  23.6 2.5 %shard_map.95 = (bf16[2,1024,512]{2,1,0:T(8,128)(2,1)S(1)}, f32[128,1024]{1,0:T(8,128)S(1)}) custom-call(f32[2,80,512]{2,1,0:T(8,128)S(1)} %get-tuple-element.32.own_ref, f32[2,80,512]{2,1,0:T(8,128)S(1)} %collective-permute-done.1.a_ref, f32[2,80,512]{2,1,0:T(8,128)S(1)} %collective-permute-done.2.b_ref, f32[2,80,512]{2,1,0:T(8,128)S(1)} %collective-permute-done.3.c_ref, ...), custom_call_target="tpu_custom_call" | custom-call | flops 1073741824 | bytes 8388608 | tf_op jit(solution)/shard_map/pallas_call | solution.py:212
  26.0 5.0 %collective-permute-done.b_ref = f32[2,80,512]{2,1,0:T(8,128)S(1)} collective-permute-done((f32[2,80,512]{2,1,0:T(8,128)S(1)}, f32[2,80,512]{2,1,0:T(8,128)S(1)}, u32[]{:S(2)}, u32[]{:S(2)}) %collective-permute-start) | collective-permute-done | bytes 327712 | tf_op jit(solution)/shard_map/ppermute | solution.py:397
  31.0 0.9 collective-permute-start.5
  31.9 0.0 collective-permute-done.4.a_ref
  31.9 1.3 %collective-permute-done.5.c_ref = f32[2,80,512]{2,1,0:T(8,128)S(1)} collective-permute-done((f32[2,80,512]{2,1,0:T(8,128)S(1)}, f32[2,80,512]{2,1,0:T(8,128)S(1)}, u32[]{:S(2)}, u32[]{:S(2)}) %collective-permute-start.5) | collective-permute-done | bytes 327712 | tf_op jit(solution)/shard_map/ppermute | solution.py:406
  33.2 2.5 %shard_map.96 = (bf16[2,1024,512]{2,1,0:T(8,128)(2,1)S(1)}, f32[128,1024]{1,0:T(8,128)S(1)}) custom-call(f32[2,80,512]{2,1,0:T(8,128)S(1)} %get-tuple-element.31.own_ref, f32[2,80,512]{2,1,0:T(8,128)S(1)} %collective-permute-done.4.a_ref, f32[2,80,512]{2,1,0:T(8,128)S(1)} %collective-permute-done.b_ref, f32[2,80,512]{2,1,0:T(8,128)S(1)} %collective-permute-done.5.c_ref, ...), custom_call_target="tpu_custom_call" | custom-call | flops 1073741824 | bytes 8388608 | tf_op jit(solution)/shard_map/pallas_call | solution.py:212
  35.7 2.4 %theirs.1 = f32[1152,512]{1,0:T(8,128)S(1)} custom-call(bf16[2,1024,512]{2,1,0:T(8,128)(2,1)S(1)} %get-tuple-element.38.refs_0_, bf16[2,1024,512]{2,1,0:T(8,128)(2,1)S(1)} %get-tuple-element.43.refs_1_, bf16[2,1024,1024]{2,1,0:T(8,128)(2,1)S(1)} %copy-done, f32[128,1024]{1,0:T(8,128)S(1)} %get-tuple-element.44.refs_3_.small_ref), custom_call_target="tpu_custom_call" | custom-call | flops 2147483648 | bytes 8388608 | tf_op jit(solution)/shard_map/theirs/pallas_call | solution.py:246
  38.0 0.5 collective-permute-start.6
  38.5 0.0 copy-done.1
  38.5 0.0 copy-done.2
  38.5 2.4 %mine.1.mine_ref = f32[1024,512]{1,0:T(8,128)S(1)} custom-call(bf16[2,1024,512]{2,1,0:T(8,128)(2,1)S(1)} %get-tuple-element.38.refs_0_, bf16[2,1024,512]{2,1,0:T(8,128)(2,1)S(1)} %get-tuple-element.43.refs_1_, bf16[2,1024,1024]{2,1,0:T(8,128)(2,1)S(1)} %copy-done), custom_call_target="tpu_custom_call" | custom-call | flops 2147483648 | bytes 8388608 | tf_op jit(solution)/shard_map/mine/pallas_call | solution.py:246
  40.9 1.8 %collective-permute-done.6.got_ref = f32[1152,512]{1,0:T(8,128)S(1)} collective-permute-done((f32[1152,512]{1,0:T(8,128)S(1)}, f32[1152,512]{1,0:T(8,128)S(1)}, u32[]{:S(2)}, u32[]{:S(2)}) %collective-permute-start.6) | collective-permute-done | bytes 2359328 | tf_op jit(solution)/shard_map/ppermute | solution.py:414
  42.7 1.7 %blocks.1 = f32[8,144,512]{2,1,0:T(8,128)} custom-call(f32[1024,512]{1,0:T(8,128)S(1)} %mine.1.mine_ref, f32[1152,512]{1,0:T(8,128)S(1)} %collective-permute-done.6.got_ref, f32[128,1024]{1,0:T(8,128)S(1)} %get-tuple-element.44.refs_3_.small_ref), custom_call_target="tpu_custom_call" | custom-call | flops 524288 | bytes 7340032 | tf_op jit(solution)/shard_map/blocks/pallas_call | solution.py:276
  44.3 7.4 %all-to-all-start = ((f32[8,144,512]{2,1,0:T(8,128)}), f32[8,144,512]{2,1,0:T(8,128)S(1)}, u32[]{:S(2)}, u32[]{:S(2)}) async-start(f32[8,144,512]{2,1,0:T(8,128)} %blocks.1), calls=%async_computation | async-start | bytes 4718592 | tf_op jit(solution)/shard_map/all_to_all | solution.py:70
  51.7 4.0 %copy.10 = bf16[1024,1024]{0,1:T(8,128)(2,1)} copy(bf16[1024,1024]{1,0:T(8,128)(2,1)} %w_any.1) | data formatting | bytes 4194304 | tf_op jit(solution)/shard_map/optimization_barrier | solution.py:416
  55.7 9.0 %latent.1 = bf16[2,1024,1024]{2,1,0:T(8,128)(2,1)} custom-call(bf16[1024,1024]{1,0:T(8,128)(2,1)} %bitcast.15, bf16[2,1024,512]{2,1,0:T(8,128)(2,1)} %copy-done.1, bf16[2,1024,512]{2,1,0:T(8,128)(2,1)} %copy-done.2), custom_call_target="tpu_custom_call" | custom-call | flops 4294967296 | bytes 8388608 | tf_op jit(solution)/shard_map/latent/pallas_call | solution.py:369
  64.7 4.7 %all-to-all-done = f32[8,144,512]{2,1,0:T(8,128)S(1)} async-done(((f32[8,144,512]{2,1,0:T(8,128)}), f32[8,144,512]{2,1,0:T(8,128)S(1)}, u32[]{:S(2)}, u32[]{:S(2)}) %all-to-all-start) | async-done | bytes 2359328 | tf_op jit(solution)/shard_map/all_to_all | solution.py:70
  69.4 0.2 reduce_sum.9
  69.7 0.1 bitcast_select_fusion
  69.8 0.1 pad_maximum_fusion
  69.9 13.0 %all_to_all.15.second_ref = f32[8,48,512]{2,1,0:T(8,128)S(1)} all-to-all(f32[8,48,512]{2,1,0:T(8,128)S(1)} %pad_maximum_fusion), channel_id=1, replica_groups={{0,64,12,76,3,67,15,79},{80,16,92,28,83,19,95,31},{4,68,8,72,7,71,11,75..., dimensions={0} | all-to-all | bytes 1572864 | tf_op jit(solution)/shard_map/all_to_all | solution.py:70
  82.8 0.1 gather.1
  82.9 13.5 %all_to_all.16.third_ref = f32[8,32,512]{2,1,0:T(8,128)S(1)} all-to-all(f32[8,32,512]{2,1,0:T(8,128)S(1)} %get-tuple-element.50), channel_id=1, replica_groups={{0,80,4,84,1,81,5,85},{64,16,68,20,65,17,69,21},{12,92,8,88,13,93,9,89}..., dimensions={0} | all-to-all | bytes 1048576 | tf_op jit(solution)/shard_map/all_to_all | solution.py:70
  96.4 2.8 %collective-permute-start.7 = (f32[160,512]{1,0:T(8,128)S(1)}, f32[160,512]{1,0:T(8,128)S(1)}, u32[]{:S(2)}, u32[]{:S(2)}) collective-permute-start(f32[160,512]{1,0:T(8,128)S(1)} %pick.1.done_ref), channel_id=1, source_target_pairs={{0,32},{1,33},{2,34},{3,35},{4,36},{5,37},{6,38},{7,39},{8,40},{9,... | collective-permute-start | bytes 983048 | tf_op jit(solution)/shard_map/ppermute | solution.py:430
  99.2 1.3 %collective-permute-done.7.other_ref = f32[160,512]{1,0:T(8,128)S(1)} collective-permute-done((f32[160,512]{1,0:T(8,128)S(1)}, f32[160,512]{1,0:T(8,128)S(1)}, u32[]{:S(2)}, u32[]{:S(2)}) %collective-permute-start.7) | collective-permute-done | bytes 327712 | tf_op jit(solution)/shard_map/ppermute | solution.py:430
  100.5 0.8 finish.1
  (8 shorter events, 0.1 us)
Async XLA Ops:
  0.6 0.9 copy-start.5
  1.5 0.7 copy-start.8
  2.2 11.8 %copy-start = (bf16[2,1024,1024]{2,1,0:T(8,128)(2,1)S(1)}, bf16[2,1024,1024]{2,1,0:T(8,128)(2,1)}, u32[]{:S(2)}) copy-start(bf16[2,1024,1024]{2,1,0:T(8,128)(2,1)} %refs_2_.3) | copy-start | bytes 12582916
  2.2 11.8 %copy-start.6 = (bf16[80,1024]{1,0:T(8,128)(2,1)S(1)}, bf16[80,1024]{1,0:T(8,128)(2,1)}, u32[]{:S(2)}) copy-start(bf16[80,1024]{1,0:T(8,128)(2,1)} %f_ref.3) | copy-start | bytes 491524
  10.6 9.9 %collective-permute-start.2 = (f32[2,80,512]{2,1,0:T(8,128)S(1)}, f32[2,80,512]{2,1,0:T(8,128)S(1)}, u32[]{:S(2)}, u32[]{:S(2)}) collective-permute-start(f32[2,80,512]{2,1,0:T(8,128)S(1)} %get-tuple-element.32.own_ref), channel_id=1, source_target_pairs={{0,64},{1,65},{2,66},{3,67},{4,68},{5,69},{6,70},{7,71},{8,72},{9,... | collective-permute-start | bytes 983048 | tf_op jit(solution)/shard_map/ppermute | solution.py:397
  13.1 10.4 %collective-permute-start.1 = (f32[2,80,512]{2,1,0:T(8,128)S(1)}, f32[2,80,512]{2,1,0:T(8,128)S(1)}, u32[]{:S(2)}, u32[]{:S(2)}) collective-permute-start(f32[2,80,512]{2,1,0:T(8,128)S(1)} %get-tuple-element.32.own_ref), channel_id=1, source_target_pairs={{0,32},{1,33},{2,34},{3,35},{4,36},{5,37},{6,38},{7,39},{8,40},{9,... | collective-permute-start | bytes 983048 | tf_op jit(solution)/shard_map/ppermute | solution.py:398
  14.1 9.4 %copy-start.3 = (f32[2,1024,512]{2,1,0:T(8,128)S(1)}, f32[2,1024,512]{2,1,0:T(8,128)}, u32[]{:S(2)}) copy-start(f32[2,1024,512]{2,1,0:T(8,128)} %get-tuple-element.35.slope_ref) | copy-start | bytes 12582916
  14.1 9.4 %copy-start.4 = (f32[80,1024]{1,0:T(8,128)S(1)}, f32[80,1024]{1,0:T(8,128)}, u32[]{:S(2)}) copy-start(f32[80,1024]{1,0:T(8,128)} %obs_ref.3) | copy-start | bytes 983044
  14.1 9.4 %copy-start.7 = (f32[1024]{0:T(1024)S(1)}, f32[1024]{0:T(1024)}, u32[]{:S(2)}) copy-start(f32[1024]{0:T(1024)} %param.8) | copy-start | bytes 12292
  20.5 3.0 %collective-permute-start.3 = (f32[2,80,512]{2,1,0:T(8,128)S(1)}, f32[2,80,512]{2,1,0:T(8,128)S(1)}, u32[]{:S(2)}, u32[]{:S(2)}) collective-permute-start(f32[2,80,512]{2,1,0:T(8,128)S(1)} %collective-permute-done.2.b_ref), channel_id=1, source_target_pairs={{0,32},{1,33},{2,34},{3,35},{4,36},{5,37},{6,38},{7,39},{8,40},{9,... | collective-permute-start | bytes 983048 | tf_op jit(solution)/shard_map/ppermute | solution.py:406
  21.8 9.3 %collective-permute-start = (f32[2,80,512]{2,1,0:T(8,128)S(1)}, f32[2,80,512]{2,1,0:T(8,128)S(1)}, u32[]{:S(2)}, u32[]{:S(2)}) collective-permute-start(f32[2,80,512]{2,1,0:T(8,128)S(1)} %get-tuple-element.31.own_ref), channel_id=1, source_target_pairs={{0,64},{1,65},{2,66},{3,67},{4,68},{5,69},{6,70},{7,71},{8,72},{9,... | collective-permute-start | bytes 983048 | tf_op jit(solution)/shard_map/ppermute | solution.py:397
  23.2 8.7 %collective-permute-start.4 = (f32[2,80,512]{2,1,0:T(8,128)S(1)}, f32[2,80,512]{2,1,0:T(8,128)S(1)}, u32[]{:S(2)}, u32[]{:S(2)}) collective-permute-start(f32[2,80,512]{2,1,0:T(8,128)S(1)} %get-tuple-element.31.own_ref), channel_id=1, source_target_pairs={{0,32},{1,33},{2,34},{3,35},{4,36},{5,37},{6,38},{7,39},{8,40},{9,... | collective-permute-start | bytes 983048 | tf_op jit(solution)/shard_map/ppermute | solution.py:398
  26.0 12.5 %copy-start.1 = (bf16[2,1024,512]{2,1,0:T(8,128)(2,1)}, bf16[2,1024,512]{2,1,0:T(8,128)(2,1)S(1)}, u32[]{:S(2)}) copy-start(bf16[2,1024,512]{2,1,0:T(8,128)(2,1)S(1)} %get-tuple-element.38.refs_0_) | copy-start | bytes 6291460
  31.0 2.1 %collective-permute-start.5 = (f32[2,80,512]{2,1,0:T(8,128)S(1)}, f32[2,80,512]{2,1,0:T(8,128)S(1)}, u32[]{:S(2)}, u32[]{:S(2)}) collective-permute-start(f32[2,80,512]{2,1,0:T(8,128)S(1)} %collective-permute-done.b_ref), channel_id=1, source_target_pairs={{0,32},{1,33},{2,34},{3,35},{4,36},{5,37},{6,38},{7,39},{8,40},{9,... | collective-permute-start | bytes 983048 | tf_op jit(solution)/shard_map/ppermute | solution.py:406
  35.6 2.9 %copy-start.2 = (bf16[2,1024,512]{2,1,0:T(8,128)(2,1)}, bf16[2,1024,512]{2,1,0:T(8,128)(2,1)S(1)}, u32[]{:S(2)}) copy-start(bf16[2,1024,512]{2,1,0:T(8,128)(2,1)S(1)} %get-tuple-element.43.refs_1_) | copy-start | bytes 6291460
  38.0 4.6 %collective-permute-start.6 = (f32[1152,512]{1,0:T(8,128)S(1)}, f32[1152,512]{1,0:T(8,128)S(1)}, u32[]{:S(2)}, u32[]{:S(2)}) collective-permute-start(f32[1152,512]{1,0:T(8,128)S(1)} %theirs.1), channel_id=1, source_target_pairs={{0,32},{1,33},{2,34},{3,35},{4,36},{5,37},{6,38},{7,39},{8,40},{9,... | collective-permute-start | bytes 7077896 | tf_op jit(solution)/shard_map/ppermute | solution.py:414
  44.3 25.1 %all-to-all-start = ((f32[8,144,512]{2,1,0:T(8,128)}), f32[8,144,512]{2,1,0:T(8,128)S(1)}, u32[]{:S(2)}, u32[]{:S(2)}) async-start(f32[8,144,512]{2,1,0:T(8,128)} %blocks.1), calls=%async_computation | async-start | bytes 4718592 | tf_op jit(solution)/shard_map/all_to_all | solution.py:70
  96.4 4.1 %collective-permute-start.7 = (f32[160,512]{1,0:T(8,128)S(1)}, f32[160,512]{1,0:T(8,128)S(1)}, u32[]{:S(2)}, u32[]{:S(2)}) collective-permute-start(f32[160,512]{1,0:T(8,128)S(1)} %pick.1.done_ref), channel_id=1, source_target_pairs={{0,32},{1,33},{2,34},{3,35},{4,36},{5,37},{6,38},{7,39},{8,40},{9,... | collective-permute-start | bytes 983048 | tf_op jit(solution)/shard_map/ppermute | solution.py:430
where the time goes:
time: 102 us; the launch traced here: 101 us
  Pallas kernels  34.5 us (34%)
  blocking collectives  26.4 us (26%)
  starting transfers between devices  18.1 us (18%)
  waiting for transfers between devices  15.5 us (15%)
  local copies, waits for them, and re-layouts  5.65 us (6%)
    all_to_all x2, blocking collectives, all_to_all(): lax.all_to_all(value, AXES, 0, 0, axis_index_groups=groups, tiled=True)  26.4 us
    pallas_call x2, Pallas kernels, forward(): pl.pallas_call(functools.partial(forward_kernel, half, first), in_specs=[...  13.2 us
    pallas_call x1, Pallas kernels, latent(): pl.pallas_call(latent_kernel, grid=(m, d // CHUNK), in_specs=[pl.BlockSpe...  8.95 us
    all_to_all x1, starting transfers between devices, all_to_all(): lax.all_to_all(value, AXES, 0, 0, axis_index_groups=groups, tiled=True)  7.4 us
    ppermute x2, waiting for transfers between devices, shards(): across = lax.ppermute(fc, AXES, SWAP_Z)  6.51 us
    pallas_call x2, Pallas kernels, backward(): pl.pallas_call(functools.partial(backward_kernel, factor, half), in_specs...  4.98 us
    pallas_call x2, Pallas kernels, weight_half(): pl.pallas_call(functools.partial(weight_kernel, bool(small)), in_specs=[V...  4.74 us
    all_to_all x1, waiting for transfers between devices, all_to_all(): lax.all_to_all(value, AXES, 0, 0, axis_index_groups=groups, tiled=True)  4.73 us
  transfers between devices with their start and end apart: 9, of which 6 were waited for; matrix products, arithmetic and copies ran while one was open for 4% of the time, Pallas kernels for 18%

commit v1 on v0

--- a/solution.py
+++ b/solution.py
@@ -83,7 +83,7 @@
 
 
 def params(mib=60):
-    return pltpu.CompilerParams(vmem_limit_bytes=mib << 20)
+    return pltpu.CompilerParams(vmem_limit_bytes=int(mib * 1048576))
 
 
 def cost(flops, bytes_accessed):
@@ -223,38 +223,36 @@
     )(*operands)
 
 
-def weight_kernel(other, *refs):
+def weight_kernel(other, begin, end, *refs):
     gps, (x_ref, *rest) = refs[:HALVES], refs[HALVES:]
     out_ref = rest[-1]
-    m, h, n = gps[0].shape
+    m, _, n = gps[0].shape
     columns = out_ref.shape[1]
     core = lax.rem(lax.axis_index("ens"), 2)
     own = pl.ds(pl.multiple_of((1 - core if other else core) * columns, columns), columns)
-    for r in range(0, h, CHUNK):
+    for r in range(begin, end, CHUNK):
         rows = pl.ds(r, CHUNK)
-        out_ref[rows, :] = sum(
+        out_ref[r - begin : r - begin + CHUNK, :] = sum(
             dot_nt(gp[i, rows, :], x_ref[i, own, k * n : (k + 1) * n]) for i in range(m) for k, gp in enumerate(gps)
         )
-    if other:
-        out_ref[h:, :] = rest[0][:, own]
-
-
-def weight_half(gps, state, *small):
+    if len(rest) > 1:
+        out_ref[end - begin :, :] = rest[0][:, own]
+
+
+def weight_half(gps, state, other, begin, end, *small):
     m, d, g = state.shape
-    h = gps[0].shape[1]
-    rows = h + sum(one.shape[0] for one in small)
-    return pl.pallas_call(
-        functools.partial(weight_kernel, bool(small)),
+    rows = end - begin + sum(one.shape[0] for one in small)
+    return pl.pallas_call(
+        functools.partial(weight_kernel, other, begin, end),
         in_specs=[VMEM] * (HALVES + 1 + len(small)),
         out_specs=VMEM,
         out_shape=jax.ShapeDtypeStruct((rows, d // 2), F32),
         compiler_params=params(16),
-        cost_estimate=cost(m * h * d * g, m * g * (2 * h + d) + 2 * h * d),
-        name="theirs" if small else "mine",
+        cost_estimate=cost(m * (end - begin) * d * g, m * g * (2 * (end - begin) + d) + 2 * rows * d),
     )(*gps, state, *small)
 
 
-def blocks_kernel(mine_ref, got_ref, small_ref, out_ref):
+def blocks_kernel(mine_ref, low_ref, high_ref, small_ref, out_ref):
     core = lax.rem(lax.axis_index("ens"), 2)
     h, columns = mine_ref.shape
     own = pl.ds(pl.multiple_of(core * columns, columns), columns)
@@ -263,25 +261,27 @@
         for place, block in enumerate(order):
             k, j = divmod(place, 8)
             rows = slice(16 * block, 16 * block + 16)
-            out_ref[k, 16 * j : 16 * j + 16, :] = mine_ref[rows, :] + got_ref[rows, :]
+            got_ref, start = (low_ref, 0) if 16 * block < h // 2 else (high_ref, h // 2)
+            got = got_ref[16 * block - start : 16 * block - start + 16, :]
+            out_ref[k, 16 * j : 16 * j + 16, :] = mine_ref[rows, :] + got
 
     pl.when(core == 0)(lambda: fill(ORDER[0]))
     pl.when(core != 0)(lambda: fill(ORDER[1]))
     for k in range(8):
         rows = slice(16 * k, 16 * k + 16)
-        out_ref[k, 128:, :] = small_ref[rows, own] + got_ref[h + 16 * k : h + 16 * k + 16, :]
-
-
-def make_blocks(mine, got, small):
+        out_ref[k, 128:, :] = small_ref[rows, own] + high_ref[h // 2 + 16 * k : h // 2 + 16 * k + 16, :]
+
+
+def make_blocks(mine, low, high, small):
     return pl.pallas_call(
         blocks_kernel,
-        in_specs=[VMEM] * 3,
+        in_specs=[VMEM] * 4,
         out_specs=VMEM,
         out_shape=jax.ShapeDtypeStruct((8, 144, 512), F32),
         compiler_params=params(16),
         cost_estimate=cost(1 << 19, 7 << 20),
         name="blocks",
-    )(mine, got, small)
+    )(mine, low, high, small)
 
 
 def gather_kernel(second_ref, out_ref, kept_ref):
@@ -410,9 +410,13 @@
         )
         init = (small,)
         gps.append(gp)
-    theirs = weight_half(gps, encoded_state, small)
-    got = lax.ppermute(theirs, AXES, SWAP_CORE)
-    blocks = make_blocks(weight_half(gps, encoded_state), got, small)
+    units = w_in.shape[0]
+    low = weight_half(gps, encoded_state, True, 0, units // 2)
+    low = lax.ppermute(low, AXES, SWAP_CORE)
+    high = weight_half(gps, encoded_state, True, units // 2, units, small)
+    high = lax.ppermute(high, AXES, SWAP_CORE)
+    own = weight_half(gps, encoded_state, False, 0, units)
+    blocks = make_blocks(own, low, high, small)
     blocks, late_weight = lax.optimization_barrier((blocks, w_in))
     first = all_to_all(blocks, CUBES[0])
     first, latent_sensitivity = lax.optimization_barrier((first, latent(late_weight.T, gps)))

time: 102 us -> 101 us (level)
  waiting for transfers between devices: 15.5 us -> 14 us
    ppermute x1 -> x2, waiting for transfers between devices: 1.79 us -> 0.29 us  [the longest x1 0.29 us: shards(): low = lax.ppermute(low, AXES, SWAP_CORE)]
    pallas_call x3 -> x4, Pallas kernels: 6.43 us -> 6.63 us  [the longest x3 4.94 us: weight_half(): pl.pallas_call(functools.partial(weight_kernel, other, begin, end), in_sp...]
  transfers between devices with their start and end apart: 9 -> 10, of which waited for: 6 -> 6; matrix products, arithmetic and copies ran while one was open for 4% -> 4% of each run, Pallas kernels for 18% -> 20%
where the time goes in v1:
time: 101 us; the launch traced here: 100 us
  Pallas kernels  34.7 us (34%)
  blocking collectives  26.5 us (26%)
  starting transfers between devices  18.3 us (18%)
  waiting for transfers between devices  14 us (14%)
  local copies, waits for them, and re-layouts  5.65 us (6%)
    all_to_all x2, blocking collectives, all_to_all(): lax.all_to_all(value, AXES, 0, 0, axis_index_groups=groups, tiled=True)  26.5 us
    pallas_call x2, Pallas kernels, forward(): pl.pallas_call(functools.partial(forward_kernel, half, first), in_specs=[...  13.2 us
    pallas_call x1, Pallas kernels, latent(): pl.pallas_call(latent_kernel, grid=(m, d // CHUNK), in_specs=[pl.BlockSpe...  8.95 us
    all_to_all x1, starting transfers between devices, all_to_all(): lax.all_to_all(value, AXES, 0, 0, axis_index_groups=groups, tiled=True)  7.4 us
    ppermute x2, waiting for transfers between devices, shards(): across = lax.ppermute(fc, AXES, SWAP_Z)  6.51 us
    pallas_call x2, Pallas kernels, backward(): pl.pallas_call(functools.partial(backward_kernel, factor, half), in_specs...  4.98 us
    pallas_call x3, Pallas kernels, weight_half(): pl.pallas_call(functools.partial(weight_kernel, other, begin, end), in_sp...  4.94 us
    all_to_all x1, waiting for transfers between devices, all_to_all(): lax.all_to_all(value, AXES, 0, 0, axis_index_groups=groups, tiled=True)  4.73 us
  transfers between devices with their start and end apart: 10, of which 6 were waited for; matrix products, arithmetic and copies ran while one was open for 4% of the time, Pallas kernels for 20%

profile of v1, /device:TPU:1, one launch (start us, length us, event | category | flops | bytes accessed | tf_op | source)
XLA Modules:
  0.0 100.2 jit_solution(10987833469354524411)
XLA Ops:
  0.6 0.0 copy-start.5
  0.6 0.9 copy-done.5
  1.6 0.7 copy-done.8
  2.2 8.3 %shard_map.93 = (bf16[2,1024,512]{2,1,0:T(8,128)(2,1)S(1)}, f32[2,1024,512]{2,1,0:T(8,128)}, f32[2,80,512]{2,1,0:T(8,128)S(1)}, bf16[1024,1024]{1,0:T(8,128)(2,1)S(1)}, f32[1024,1]{1,0:T(8,128)S(1)}) custom-call(bf16[2,1024,1024]{2,1,0:T(8,128)(2,1)} %refs_2_.5, bf16[1024,1024]{1,0:T(8,128)(2,1)} %w_any.1, f32[8,128]{1,0:T(8,128)S(1)} %bitcast.12, ...), custom_call_target="tpu_custom_call" | custom-call | flops 2315255808 | bytes 8388608 | tf_op jit(solution)/shard_map/pallas_call | solution.py:159
  10.6 2.5 %collective-permute-start.2 = (f32[2,80,512]{2,1,0:T(8,128)S(1)}, f32[2,80,512]{2,1,0:T(8,128)S(1)}, u32[]{:S(2)}, u32[]{:S(2)}) collective-permute-start(f32[2,80,512]{2,1,0:T(8,128)S(1)} %get-tuple-element.32.own_ref), channel_id=1, source_target_pairs={{0,64},{1,65},{2,66},{3,67},{4,68},{5,69},{6,70},{7,71},{8,72},{9,... | collective-permute-start | bytes 983048 | tf_op jit(solution)/shard_map/ppermute | solution.py:397
  13.1 1.0 collective-permute-start.1
  14.1 0.0 copy-done
  14.1 0.0 copy-done.6
  14.1 0.0 copy-start.7
  14.1 4.9 %shard_map.94 = (bf16[2,1024,512]{2,1,0:T(8,128)(2,1)S(1)}, f32[2,1024,512]{2,1,0:T(8,128)S(1)}, f32[2,80,512]{2,1,0:T(8,128)S(1)}) custom-call(bf16[2,1024,1024]{2,1,0:T(8,128)(2,1)S(1)} %copy-done, bf16[1024,1024]{1,0:T(8,128)(2,1)S(1)} %get-tuple-element.29.w_any, f32[1024,1]{1,0:T(8,128)S(1)} %get-tuple-element.30.b_any, bf16[80,1024]{1,0:T(8,128)(2,1)S(1)} %copy-done.6), custom_call_target="tpu_custom_call" | custom-call | flops 2315255808 | bytes 8388608 | tf_op jit(solution)/shard_map/pallas_call | solution.py:159
  19.0 1.5 %collective-permute-done.2.b_ref = f32[2,80,512]{2,1,0:T(8,128)S(1)} collective-permute-done((f32[2,80,512]{2,1,0:T(8,128)S(1)}, f32[2,80,512]{2,1,0:T(8,128)S(1)}, u32[]{:S(2)}, u32[]{:S(2)}) %collective-permute-start.2) | collective-permute-done | bytes 327712 | tf_op jit(solution)/shard_map/ppermute | solution.py:397
  20.5 1.3 %collective-permute-start.3 = (f32[2,80,512]{2,1,0:T(8,128)S(1)}, f32[2,80,512]{2,1,0:T(8,128)S(1)}, u32[]{:S(2)}, u32[]{:S(2)}) collective-permute-start(f32[2,80,512]{2,1,0:T(8,128)S(1)} %collective-permute-done.2.b_ref), channel_id=1, source_target_pairs={{0,32},{1,33},{2,34},{3,35},{4,36},{5,37},{6,38},{7,39},{8,40},{9,... | collective-permute-start | bytes 983048 | tf_op jit(solution)/shard_map/ppermute | solution.py:406
  21.8 1.5 %collective-permute-start = (f32[2,80,512]{2,1,0:T(8,128)S(1)}, f32[2,80,512]{2,1,0:T(8,128)S(1)}, u32[]{:S(2)}, u32[]{:S(2)}) collective-permute-start(f32[2,80,512]{2,1,0:T(8,128)S(1)} %get-tuple-element.31.own_ref), channel_id=1, source_target_pairs={{0,64},{1,65},{2,66},{3,67},{4,68},{5,69},{6,70},{7,71},{8,72},{9,... | collective-permute-start | bytes 983048 | tf_op jit(solution)/shard_map/ppermute | solution.py:397
  23.2 0.3 collective-permute-start.4
  23.5 0.0 collective-permute-done.1.a_ref
  23.5 0.0 collective-permute-done.3.c_ref
  23.5 0.0 copy-done.3
  23.5 0.0 copy-done.4
  23.5 0.0 copy-done.7
  23.6 2.5 %shard_map.95 = (bf16[2,1024,512]{2,1,0:T(8,128)(2,1)S(1)}, f32[128,1024]{1,0:T(8,128)S(1)}) custom-call(f32[2,80,512]{2,1,0:T(8,128)S(1)} %get-tuple-element.32.own_ref, f32[2,80,512]{2,1,0:T(8,128)S(1)} %collective-permute-done.1.a_ref, f32[2,80,512]{2,1,0:T(8,128)S(1)} %collective-permute-done.2.b_ref, f32[2,80,512]{2,1,0:T(8,128)S(1)} %collective-permute-done.3.c_ref, ...), custom_call_target="tpu_custom_call" | custom-call | flops 1073741824 | bytes 8388608 | tf_op jit(solution)/shard_map/pallas_call | solution.py:212
  26.0 5.0 %collective-permute-done.b_ref = f32[2,80,512]{2,1,0:T(8,128)S(1)} collective-permute-done((f32[2,80,512]{2,1,0:T(8,128)S(1)}, f32[2,80,512]{2,1,0:T(8,128)S(1)}, u32[]{:S(2)}, u32[]{:S(2)}) %collective-permute-start) | collective-permute-done | bytes 327712 | tf_op jit(solution)/shard_map/ppermute | solution.py:397
  31.0 0.9 collective-permute-start.5
  31.9 0.0 collective-permute-done.4.a_ref
  31.9 1.3 %collective-permute-done.5.c_ref = f32[2,80,512]{2,1,0:T(8,128)S(1)} collective-permute-done((f32[2,80,512]{2,1,0:T(8,128)S(1)}, f32[2,80,512]{2,1,0:T(8,128)S(1)}, u32[]{:S(2)}, u32[]{:S(2)}) %collective-permute-start.5) | collective-permute-done | bytes 327712 | tf_op jit(solution)/shard_map/ppermute | solution.py:406
  33.2 2.5 %shard_map.96 = (bf16[2,1024,512]{2,1,0:T(8,128)(2,1)S(1)}, f32[128,1024]{1,0:T(8,128)S(1)}) custom-call(f32[2,80,512]{2,1,0:T(8,128)S(1)} %get-tuple-element.31.own_ref, f32[2,80,512]{2,1,0:T(8,128)S(1)} %collective-permute-done.4.a_ref, f32[2,80,512]{2,1,0:T(8,128)S(1)} %collective-permute-done.b_ref, f32[2,80,512]{2,1,0:T(8,128)S(1)} %collective-permute-done.5.c_ref, ...), custom_call_target="tpu_custom_call" | custom-call | flops 1073741824 | bytes 8388608 | tf_op jit(solution)/shard_map/pallas_call | solution.py:212
  35.7 1.3 %shard_map.99 = f32[640,512]{1,0:T(8,128)S(1)} custom-call(bf16[2,1024,512]{2,1,0:T(8,128)(2,1)S(1)} %get-tuple-element.38.refs_0_, bf16[2,1024,512]{2,1,0:T(8,128)(2,1)S(1)} %get-tuple-element.43.refs_1_, bf16[2,1024,1024]{2,1,0:T(8,128)(2,1)S(1)} %copy-done, f32[128,1024]{1,0:T(8,128)S(1)} %get-tuple-element.44.refs_3_.small_ref), custom_call_target="tpu_custom_call" | custom-call | flops 1073741824 | bytes 5505024 | tf_op jit(solution)/shard_map/pallas_call | solution.py:245
  37.0 0.5 collective-permute-start.7
  37.4 1.3 %shard_map.98 = f32[512,512]{1,0:T(8,128)S(1)} custom-call(bf16[2,1024,512]{2,1,0:T(8,128)(2,1)S(1)} %get-tuple-element.38.refs_0_, bf16[2,1024,512]{2,1,0:T(8,128)(2,1)S(1)} %get-tuple-element.43.refs_1_, bf16[2,1024,1024]{2,1,0:T(8,128)(2,1)S(1)} %copy-done), custom_call_target="tpu_custom_call" | custom-call | flops 1073741824 | bytes 5242880 | tf_op jit(solution)/shard_map/pallas_call | solution.py:245
  38.7 0.2 collective-permute-start.6
  38.9 0.0 copy-done.1
  38.9 0.0 copy-done.2
  38.9 2.4 %shard_map.97.mine_ref = f32[1024,512]{1,0:T(8,128)S(1)} custom-call(bf16[2,1024,512]{2,1,0:T(8,128)(2,1)S(1)} %get-tuple-element.38.refs_0_, bf16[2,1024,512]{2,1,0:T(8,128)(2,1)S(1)} %get-tuple-element.43.refs_1_, bf16[2,1024,1024]{2,1,0:T(8,128)(2,1)S(1)} %copy-done), custom_call_target="tpu_custom_call" | custom-call | flops 2147483648 | bytes 8388608 | tf_op jit(solution)/shard_map/pallas_call | solution.py:245
  41.3 0.3 collective-permute-done.6.low_ref
  41.6 0.0 collective-permute-done.7.high_ref
  41.6 1.7 %blocks.1 = f32[8,144,512]{2,1,0:T(8,128)} custom-call(f32[1024,512]{1,0:T(8,128)S(1)} %shard_map.97.mine_ref, f32[512,512]{1,0:T(8,128)S(1)} %collective-permute-done.6.low_ref, f32[640,512]{1,0:T(8,128)S(1)} %collective-permute-done.7.high_ref, f32[128,1024]{1,0:T(8,128)S(1)} %get-tuple-element.44.refs_3_.small_ref), custom_call_target="tpu_custom_call" | custom-call | flops 524288 | bytes 7340032 | tf_op jit(solution)/shard_map/blocks/pallas_call | solution.py:276
  43.3 7.4 %all-to-all-start = ((f32[8,144,512]{2,1,0:T(8,128)}), f32[8,144,512]{2,1,0:T(8,128)S(1)}, u32[]{:S(2)}, u32[]{:S(2)}) async-start(f32[8,144,512]{2,1,0:T(8,128)} %blocks.1), calls=%async_computation | async-start | bytes 4718592 | tf_op jit(solution)/shard_map/all_to_all | solution.py:70
  50.7 4.0 %copy.10 = bf16[1024,1024]{0,1:T(8,128)(2,1)} copy(bf16[1024,1024]{1,0:T(8,128)(2,1)} %w_any.1) | data formatting | bytes 4194304 | tf_op jit(solution)/shard_map/optimization_barrier | solution.py:420
  54.6 9.0 %latent.1 = bf16[2,1024,1024]{2,1,0:T(8,128)(2,1)} custom-call(bf16[1024,1024]{1,0:T(8,128)(2,1)} %bitcast.15, bf16[2,1024,512]{2,1,0:T(8,128)(2,1)} %copy-done.1, bf16[2,1024,512]{2,1,0:T(8,128)(2,1)} %copy-done.2), custom_call_target="tpu_custom_call" | custom-call | flops 4294967296 | bytes 8388608 | tf_op jit(solution)/shard_map/latent/pallas_call | solution.py:369
  63.6 4.7 %all-to-all-done = f32[8,144,512]{2,1,0:T(8,128)S(1)} async-done(((f32[8,144,512]{2,1,0:T(8,128)}), f32[8,144,512]{2,1,0:T(8,128)S(1)}, u32[]{:S(2)}, u32[]{:S(2)}) %all-to-all-start) | async-done | bytes 2359328 | tf_op jit(solution)/shard_map/all_to_all | solution.py:70
  68.3 0.2 reduce_sum.9
  68.6 0.1 bitcast_select_fusion
  68.7 0.1 pad_maximum_fusion
  68.8 13.0 %all_to_all.15.second_ref = f32[8,48,512]{2,1,0:T(8,128)S(1)} all-to-all(f32[8,48,512]{2,1,0:T(8,128)S(1)} %pad_maximum_fusion), channel_id=1, replica_groups={{0,64,12,76,3,67,15,79},{80,16,92,28,83,19,95,31},{4,68,8,72,7,71,11,75..., dimensions={0} | all-to-all | bytes 1572864 | tf_op jit(solution)/shard_map/all_to_all | solution.py:70
  81.7 0.1 gather.1
  81.8 13.5 %all_to_all.16.third_ref = f32[8,32,512]{2,1,0:T(8,128)S(1)} all-to-all(f32[8,32,512]{2,1,0:T(8,128)S(1)} %get-tuple-element.50), channel_id=1, replica_groups={{0,80,4,84,1,81,5,85},{64,16,68,20,65,17,69,21},{12,92,8,88,13,93,9,89}..., dimensions={0} | all-to-all | bytes 1048576 | tf_op jit(solution)/shard_map/all_to_all | solution.py:70
  95.3 2.8 %collective-permute-start.8 = (f32[160,512]{1,0:T(8,128)S(1)}, f32[160,512]{1,0:T(8,128)S(1)}, u32[]{:S(2)}, u32[]{:S(2)}) collective-permute-start(f32[160,512]{1,0:T(8,128)S(1)} %pick.1.done_ref), channel_id=1, source_target_pairs={{0,32},{1,33},{2,34},{3,35},{4,36},{5,37},{6,38},{7,39},{8,40},{9,... | collective-permute-start | bytes 983048 | tf_op jit(solution)/shard_map/ppermute | solution.py:434
  98.1 1.3 %collective-permute-done.8.other_ref = f32[160,512]{1,0:T(8,128)S(1)} collective-permute-done((f32[160,512]{1,0:T(8,128)S(1)}, f32[160,512]{1,0:T(8,128)S(1)}, u32[]{:S(2)}, u32[]{:S(2)}) %collective-permute-start.8) | collective-permute-done | bytes 327712 | tf_op jit(solution)/shard_map/ppermute | solution.py:434
  99.4 0.8 finish.1
  (11 shorter events, 0.1 us)
Async XLA Ops:
  0.6 0.9 copy-start.5
  1.5 0.7 copy-start.8
  2.2 11.8 %copy-start = (bf16[2,1024,1024]{2,1,0:T(8,128)(2,1)S(1)}, bf16[2,1024,1024]{2,1,0:T(8,128)(2,1)}, u32[]{:S(2)}) copy-start(bf16[2,1024,1024]{2,1,0:T(8,128)(2,1)} %refs_2_.5) | copy-start | bytes 12582916
  2.2 11.8 %copy-start.6 = (bf16[80,1024]{1,0:T(8,128)(2,1)S(1)}, bf16[80,1024]{1,0:T(8,128)(2,1)}, u32[]{:S(2)}) copy-start(bf16[80,1024]{1,0:T(8,128)(2,1)} %f_ref.3) | copy-start | bytes 491524
  10.6 9.9 %collective-permute-start.2 = (f32[2,80,512]{2,1,0:T(8,128)S(1)}, f32[2,80,512]{2,1,0:T(8,128)S(1)}, u32[]{:S(2)}, u32[]{:S(2)}) collective-permute-start(f32[2,80,512]{2,1,0:T(8,128)S(1)} %get-tuple-element.32.own_ref), channel_id=1, source_target_pairs={{0,64},{1,65},{2,66},{3,67},{4,68},{5,69},{6,70},{7,71},{8,72},{9,... | collective-permute-start | bytes 983048 | tf_op jit(solution)/shard_map/ppermute | solution.py:397
  13.1 10.4 %collective-permute-start.1 = (f32[2,80,512]{2,1,0:T(8,128)S(1)}, f32[2,80,512]{2,1,0:T(8,128)S(1)}, u32[]{:S(2)}, u32[]{:S(2)}) collective-permute-start(f32[2,80,512]{2,1,0:T(8,128)S(1)} %get-tuple-element.32.own_ref), channel_id=1, source_target_pairs={{0,32},{1,33},{2,34},{3,35},{4,36},{5,37},{6,38},{7,39},{8,40},{9,... | collective-permute-start | bytes 983048 | tf_op jit(solution)/shard_map/ppermute | solution.py:398
  14.1 9.4 %copy-start.3 = (f32[2,1024,512]{2,1,0:T(8,128)S(1)}, f32[2,1024,512]{2,1,0:T(8,128)}, u32[]{:S(2)}) copy-start(f32[2,1024,512]{2,1,0:T(8,128)} %get-tuple-element.35.slope_ref) | copy-start | bytes 12582916
  14.1 9.4 %copy-start.4 = (f32[80,1024]{1,0:T(8,128)S(1)}, f32[80,1024]{1,0:T(8,128)}, u32[]{:S(2)}) copy-start(f32[80,1024]{1,0:T(8,128)} %obs_ref.3) | copy-start | bytes 983044
  14.1 9.4 %copy-start.7 = (f32[1024]{0:T(1024)S(1)}, f32[1024]{0:T(1024)}, u32[]{:S(2)}) copy-start(f32[1024]{0:T(1024)} %param.8) | copy-start | bytes 12292
  20.5 3.0 %collective-permute-start.3 = (f32[2,80,512]{2,1,0:T(8,128)S(1)}, f32[2,80,512]{2,1,0:T(8,128)S(1)}, u32[]{:S(2)}, u32[]{:S(2)}) collective-permute-start(f32[2,80,512]{2,1,0:T(8,128)S(1)} %collective-permute-done.2.b_ref), channel_id=1, source_target_pairs={{0,32},{1,33},{2,34},{3,35},{4,36},{5,37},{6,38},{7,39},{8,40},{9,... | collective-permute-start | bytes 983048 | tf_op jit(solution)/shard_map/ppermute | solution.py:406
  21.8 9.3 %collective-permute-start = (f32[2,80,512]{2,1,0:T(8,128)S(1)}, f32[2,80,512]{2,1,0:T(8,128)S(1)}, u32[]{:S(2)}, u32[]{:S(2)}) collective-permute-start(f32[2,80,512]{2,1,0:T(8,128)S(1)} %get-tuple-element.31.own_ref), channel_id=1, source_target_pairs={{0,64},{1,65},{2,66},{3,67},{4,68},{5,69},{6,70},{7,71},{8,72},{9,... | collective-permute-start | bytes 983048 | tf_op jit(solution)/shard_map/ppermute | solution.py:397
  23.2 8.7 %collective-permute-start.4 = (f32[2,80,512]{2,1,0:T(8,128)S(1)}, f32[2,80,512]{2,1,0:T(8,128)S(1)}, u32[]{:S(2)}, u32[]{:S(2)}) collective-permute-start(f32[2,80,512]{2,1,0:T(8,128)S(1)} %get-tuple-element.31.own_ref), channel_id=1, source_target_pairs={{0,32},{1,33},{2,34},{3,35},{4,36},{5,37},{6,38},{7,39},{8,40},{9,... | collective-permute-start | bytes 983048 | tf_op jit(solution)/shard_map/ppermute | solution.py:398
  26.0 12.9 %copy-start.1 = (bf16[2,1024,512]{2,1,0:T(8,128)(2,1)}, bf16[2,1024,512]{2,1,0:T(8,128)(2,1)S(1)}, u32[]{:S(2)}) copy-start(bf16[2,1024,512]{2,1,0:T(8,128)(2,1)S(1)} %get-tuple-element.38.refs_0_) | copy-start | bytes 6291460
  31.0 2.1 %collective-permute-start.5 = (f32[2,80,512]{2,1,0:T(8,128)S(1)}, f32[2,80,512]{2,1,0:T(8,128)S(1)}, u32[]{:S(2)}, u32[]{:S(2)}) collective-permute-start(f32[2,80,512]{2,1,0:T(8,128)S(1)} %collective-permute-done.b_ref), channel_id=1, source_target_pairs={{0,32},{1,33},{2,34},{3,35},{4,36},{5,37},{6,38},{7,39},{8,40},{9,... | collective-permute-start | bytes 983048 | tf_op jit(solution)/shard_map/ppermute | solution.py:406
  35.6 3.3 %copy-start.2 = (bf16[2,1024,512]{2,1,0:T(8,128)(2,1)}, bf16[2,1024,512]{2,1,0:T(8,128)(2,1)S(1)}, u32[]{:S(2)}) copy-start(bf16[2,1024,512]{2,1,0:T(8,128)(2,1)S(1)} %get-tuple-element.43.refs_1_) | copy-start | bytes 6291460
  37.0 4.6 %collective-permute-start.7 = (f32[640,512]{1,0:T(8,128)S(1)}, f32[640,512]{1,0:T(8,128)S(1)}, u32[]{:S(2)}, u32[]{:S(2)}) collective-permute-start(f32[640,512]{1,0:T(8,128)S(1)} %shard_map.99), channel_id=1, source_target_pairs={{0,32},{1,33},{2,34},{3,35},{4,36},{5,37},{6,38},{7,39},{8,40},{9,... | collective-permute-start | bytes 3932168 | tf_op jit(solution)/shard_map/ppermute | solution.py:417
  38.7 2.9 %collective-permute-start.6 = (f32[512,512]{1,0:T(8,128)S(1)}, f32[512,512]{1,0:T(8,128)S(1)}, u32[]{:S(2)}, u32[]{:S(2)}) collective-permute-start(f32[512,512]{1,0:T(8,128)S(1)} %shard_map.98), channel_id=1, source_target_pairs={{0,32},{1,33},{2,34},{3,35},{4,36},{5,37},{6,38},{7,39},{8,40},{9,... | collective-permute-start | bytes 3145736 | tf_op jit(solution)/shard_map/ppermute | solution.py:415
  43.3 25.1 %all-to-all-start = ((f32[8,144,512]{2,1,0:T(8,128)}), f32[8,144,512]{2,1,0:T(8,128)S(1)}, u32[]{:S(2)}, u32[]{:S(2)}) async-start(f32[8,144,512]{2,1,0:T(8,128)} %blocks.1), calls=%async_computation | async-start | bytes 4718592 | tf_op jit(solution)/shard_map/all_to_all | solution.py:70
  95.3 4.1 %collective-permute-start.8 = (f32[160,512]{1,0:T(8,128)S(1)}, f32[160,512]{1,0:T(8,128)S(1)}, u32[]{:S(2)}, u32[]{:S(2)}) collective-permute-start(f32[160,512]{1,0:T(8,128)S(1)} %pick.1.done_ref), channel_id=1, source_target_pairs={{0,32},{1,33},{2,34},{3,35},{4,36},{5,37},{6,38},{7,39},{8,40},{9,... | collective-permute-start | bytes 983048 | tf_op jit(solution)/shard_map/ppermute | solution.py:434

commit v2 on v1

--- a/solution.py
+++ b/solution.py
@@ -17,6 +17,7 @@
 ROOT = math.sqrt(2.0 / math.pi)
 CUBIC = 0.044715
 CHUNK = 512
+ROWS = 1024
 FIRST, LATER = 48, 36
 
 
@@ -91,7 +92,7 @@
 
 
 def forward_rows(i, r, x, w_ref, column_ref, f_ref, hidden_ref, slope_ref):
-    rows = pl.ds(r, CHUNK)
+    rows = pl.ds(r, ROWS)
     v = dot(w_ref[rows, :], x) + column_ref[rows, :]
     v2 = v * v
     t = jnp.tanh(v * (ROOT * CUBIC * v2 + ROOT))
@@ -104,7 +105,7 @@
 
 def forward_kernel(half, first, x_any, w_any, b_any, f_any, hidden_ref, slope_ref, fc_ref, *refs):
     m, h, n = hidden_ref.shape
-    starts = range(0, h, CHUNK)
+    starts = range(0, h, ROWS)
     if first:
         w_ref, column_ref, x_ref, b_ref, f_ref, sems = refs
     else:
@@ -116,7 +117,7 @@
     fetch_x = [copy(x_any.at[i, :, pl.ds(half * n, n)], x_ref.at[i], i) for i in range(m)]
     if first:
         fetch_b, fetch_f = copy(b_any, b_ref, m), copy(f_any, f_ref, m + 1)
-        fetch_w = [copy(w_any.at[pl.ds(r, CHUNK)], w_ref.at[pl.ds(r, CHUNK)], m + 2 + j) for j, r in enumerate(starts)]
+        fetch_w = [copy(w_any.at[pl.ds(r, ROWS)], w_ref.at[pl.ds(r, ROWS)], m + 2 + j) for j, r in enumerate(starts)]
         for one in [fetch_b] + fetch_w[:1] + fetch_x[:1] + [fetch_f] + fetch_w[1:] + fetch_x[1:]:
             one.start()
         fetch_b.wait()
@@ -161,7 +162,7 @@
         in_specs=[HBM] * 4 if first else [HBM] + [VMEM] * 3,
         out_specs=[VMEM] * len(results),
         out_shape=results,
-        scratch_shapes=scratch + [pltpu.SemaphoreType.DMA((m + 2 + h // CHUNK,))],
+        scratch_shapes=scratch + [pltpu.SemaphoreType.DMA((m + 2 + h // ROWS,))],
         compiler_params=params(FIRST if first else LATER),
         cost_estimate=cost(2 * m * h * n * (d + c), m * n * (2 * d + 6 * h)),
     )(state, w_in, bias, final_matrix)

time: 101 us -> 101 us (level)
  no operation moved by 1% of the time
where the time goes in v2:
time: 101 us; the launch traced here: 100 us
  Pallas kernels  35 us (35%)
  blocking collectives  26.4 us (26%)
  starting transfers between devices  18.2 us (18%)
  waiting for transfers between devices  14 us (14%)
  local copies, waits for them, and re-layouts  5.65 us (6%)
    all_to_all x2, blocking collectives, all_to_all(): lax.all_to_all(value, AXES, 0, 0, axis_index_groups=groups, tiled=True)  26.4 us
    pallas_call x2, Pallas kernels, forward(): pl.pallas_call(functools.partial(forward_kernel, half, first), in_specs=[...  13.6 us
    pallas_call x1, Pallas kernels, latent(): pl.pallas_call(latent_kernel, grid=(m, d // CHUNK), in_specs=[pl.BlockSpe...  8.95 us
    all_to_all x1, starting transfers between devices, all_to_all(): lax.all_to_all(value, AXES, 0, 0, axis_index_groups=groups, tiled=True)  7.38 us
    ppermute x2, waiting for transfers between devices, shards(): across = lax.ppermute(fc, AXES, SWAP_Z)  6.43 us
    pallas_call x2, Pallas kernels, backward(): pl.pallas_call(functools.partial(backward_kernel, factor, half), in_specs...  4.99 us
    pallas_call x3, Pallas kernels, weight_half(): pl.pallas_call(functools.partial(weight_kernel, other, begin, end), in_sp...  4.94 us
    all_to_all x1, waiting for transfers between devices, all_to_all(): lax.all_to_all(value, AXES, 0, 0, axis_index_groups=groups, tiled=True)  4.73 us
  transfers between devices with their start and end apart: 10, of which 6 were waited for; matrix products, arithmetic and copies ran while one was open for 4% of the time, Pallas kernels for 20%

profile of v2, /device:TPU:1, one launch (start us, length us, event | category | flops | bytes accessed | tf_op | source)
XLA Modules:
  0.0 100.5 jit_solution(7611581468661072420)
XLA Ops:
  0.6 0.0 copy-start.5
  0.6 0.9 copy-done.5
  1.6 0.7 copy-done.8
  2.2 8.6 %shard_map.93 = (bf16[2,1024,512]{2,1,0:T(8,128)(2,1)S(1)}, f32[2,1024,512]{2,1,0:T(8,128)}, f32[2,80,512]{2,1,0:T(8,128)S(1)}, bf16[1024,1024]{1,0:T(8,128)(2,1)S(1)}, f32[1024,1]{1,0:T(8,128)S(1)}) custom-call(bf16[2,1024,1024]{2,1,0:T(8,128)(2,1)} %refs_2_.5, bf16[1024,1024]{1,0:T(8,128)(2,1)} %w_any.1, f32[8,128]{1,0:T(8,128)S(1)} %bitcast.12, ...), custom_call_target="tpu_custom_call" | custom-call | flops 2315255808 | bytes 8388608 | tf_op jit(solution)/shard_map/pallas_call | solution.py:160
  10.8 2.5 %collective-permute-start.2 = (f32[2,80,512]{2,1,0:T(8,128)S(1)}, f32[2,80,512]{2,1,0:T(8,128)S(1)}, u32[]{:S(2)}, u32[]{:S(2)}) collective-permute-start(f32[2,80,512]{2,1,0:T(8,128)S(1)} %get-tuple-element.32.own_ref), channel_id=1, source_target_pairs={{0,64},{1,65},{2,66},{3,67},{4,68},{5,69},{6,70},{7,71},{8,72},{9,... | collective-permute-start | bytes 983048 | tf_op jit(solution)/shard_map/ppermute | solution.py:398
  13.4 1.0 collective-permute-start.1
  14.3 0.0 copy-done
  14.3 0.0 copy-done.6
  14.3 0.0 copy-start.7
  14.3 5.0 %shard_map.94 = (bf16[2,1024,512]{2,1,0:T(8,128)(2,1)S(1)}, f32[2,1024,512]{2,1,0:T(8,128)S(1)}, f32[2,80,512]{2,1,0:T(8,128)S(1)}) custom-call(bf16[2,1024,1024]{2,1,0:T(8,128)(2,1)S(1)} %copy-done, bf16[1024,1024]{1,0:T(8,128)(2,1)S(1)} %get-tuple-element.29.w_any, f32[1024,1]{1,0:T(8,128)S(1)} %get-tuple-element.30.b_any, bf16[80,1024]{1,0:T(8,128)(2,1)S(1)} %copy-done.6), custom_call_target="tpu_custom_call" | custom-call | flops 2315255808 | bytes 8388608 | tf_op jit(solution)/shard_map/pallas_call | solution.py:160
  19.4 1.4 %collective-permute-done.2.b_ref = f32[2,80,512]{2,1,0:T(8,128)S(1)} collective-permute-done((f32[2,80,512]{2,1,0:T(8,128)S(1)}, f32[2,80,512]{2,1,0:T(8,128)S(1)}, u32[]{:S(2)}, u32[]{:S(2)}) %collective-permute-start.2) | collective-permute-done | bytes 327712 | tf_op jit(solution)/shard_map/ppermute | solution.py:398
  20.8 1.3 %collective-permute-start.3 = (f32[2,80,512]{2,1,0:T(8,128)S(1)}, f32[2,80,512]{2,1,0:T(8,128)S(1)}, u32[]{:S(2)}, u32[]{:S(2)}) collective-permute-start(f32[2,80,512]{2,1,0:T(8,128)S(1)} %collective-permute-done.2.b_ref), channel_id=1, source_target_pairs={{0,32},{1,33},{2,34},{3,35},{4,36},{5,37},{6,38},{7,39},{8,40},{9,... | collective-permute-start | bytes 983048 | tf_op jit(solution)/shard_map/ppermute | solution.py:407
  22.0 1.5 %collective-permute-start = (f32[2,80,512]{2,1,0:T(8,128)S(1)}, f32[2,80,512]{2,1,0:T(8,128)S(1)}, u32[]{:S(2)}, u32[]{:S(2)}) collective-permute-start(f32[2,80,512]{2,1,0:T(8,128)S(1)} %get-tuple-element.31.own_ref), channel_id=1, source_target_pairs={{0,64},{1,65},{2,66},{3,67},{4,68},{5,69},{6,70},{7,71},{8,72},{9,... | collective-permute-start | bytes 983048 | tf_op jit(solution)/shard_map/ppermute | solution.py:398
  23.5 0.3 collective-permute-start.4
  23.8 0.0 collective-permute-done.1.a_ref
  23.8 0.0 collective-permute-done.3.c_ref
  23.8 0.0 copy-done.3
  23.8 0.0 copy-done.4
  23.8 0.0 copy-done.7
  23.8 2.5 %shard_map.95 = (bf16[2,1024,512]{2,1,0:T(8,128)(2,1)S(1)}, f32[128,1024]{1,0:T(8,128)S(1)}) custom-call(f32[2,80,512]{2,1,0:T(8,128)S(1)} %get-tuple-element.32.own_ref, f32[2,80,512]{2,1,0:T(8,128)S(1)} %collective-permute-done.1.a_ref, f32[2,80,512]{2,1,0:T(8,128)S(1)} %collective-permute-done.2.b_ref, f32[2,80,512]{2,1,0:T(8,128)S(1)} %collective-permute-done.3.c_ref, ...), custom_call_target="tpu_custom_call" | custom-call | flops 1073741824 | bytes 8388608 | tf_op jit(solution)/shard_map/pallas_call | solution.py:213
  26.3 5.0 %collective-permute-done.b_ref = f32[2,80,512]{2,1,0:T(8,128)S(1)} collective-permute-done((f32[2,80,512]{2,1,0:T(8,128)S(1)}, f32[2,80,512]{2,1,0:T(8,128)S(1)}, u32[]{:S(2)}, u32[]{:S(2)}) %collective-permute-start) | collective-permute-done | bytes 327712 | tf_op jit(solution)/shard_map/ppermute | solution.py:398
  31.3 0.9 collective-permute-start.5
  32.2 0.0 collective-permute-done.4.a_ref
  32.2 1.3 %collective-permute-done.5.c_ref = f32[2,80,512]{2,1,0:T(8,128)S(1)} collective-permute-done((f32[2,80,512]{2,1,0:T(8,128)S(1)}, f32[2,80,512]{2,1,0:T(8,128)S(1)}, u32[]{:S(2)}, u32[]{:S(2)}) %collective-permute-start.5) | collective-permute-done | bytes 327712 | tf_op jit(solution)/shard_map/ppermute | solution.py:407
  33.4 2.5 %shard_map.96 = (bf16[2,1024,512]{2,1,0:T(8,128)(2,1)S(1)}, f32[128,1024]{1,0:T(8,128)S(1)}) custom-call(f32[2,80,512]{2,1,0:T(8,128)S(1)} %get-tuple-element.31.own_ref, f32[2,80,512]{2,1,0:T(8,128)S(1)} %collective-permute-done.4.a_ref, f32[2,80,512]{2,1,0:T(8,128)S(1)} %collective-permute-done.b_ref, f32[2,80,512]{2,1,0:T(8,128)S(1)} %collective-permute-done.5.c_ref, ...), custom_call_target="tpu_custom_call" | custom-call | flops 1073741824 | bytes 8388608 | tf_op jit(solution)/shard_map/pallas_call | solution.py:213
  35.9 1.3 %shard_map.99 = f32[640,512]{1,0:T(8,128)S(1)} custom-call(bf16[2,1024,512]{2,1,0:T(8,128)(2,1)S(1)} %get-tuple-element.38.refs_0_, bf16[2,1024,512]{2,1,0:T(8,128)(2,1)S(1)} %get-tuple-element.43.refs_1_, bf16[2,1024,1024]{2,1,0:T(8,128)(2,1)S(1)} %copy-done, f32[128,1024]{1,0:T(8,128)S(1)} %get-tuple-element.44.refs_3_.small_ref), custom_call_target="tpu_custom_call" | custom-call | flops 1073741824 | bytes 5505024 | tf_op jit(solution)/shard_map/pallas_call | solution.py:246
  37.2 0.5 collective-permute-start.7
  37.7 1.3 %shard_map.98 = f32[512,512]{1,0:T(8,128)S(1)} custom-call(bf16[2,1024,512]{2,1,0:T(8,128)(2,1)S(1)} %get-tuple-element.38.refs_0_, bf16[2,1024,512]{2,1,0:T(8,128)(2,1)S(1)} %get-tuple-element.43.refs_1_, bf16[2,1024,1024]{2,1,0:T(8,128)(2,1)S(1)} %copy-done), custom_call_target="tpu_custom_call" | custom-call | flops 1073741824 | bytes 5242880 | tf_op jit(solution)/shard_map/pallas_call | solution.py:246
  39.0 0.2 collective-permute-start.6
  39.2 0.0 copy-done.1
  39.2 0.0 copy-done.2
  39.2 2.4 %shard_map.97.mine_ref = f32[1024,512]{1,0:T(8,128)S(1)} custom-call(bf16[2,1024,512]{2,1,0:T(8,128)(2,1)S(1)} %get-tuple-element.38.refs_0_, bf16[2,1024,512]{2,1,0:T(8,128)(2,1)S(1)} %get-tuple-element.43.refs_1_, bf16[2,1024,1024]{2,1,0:T(8,128)(2,1)S(1)} %copy-done), custom_call_target="tpu_custom_call" | custom-call | flops 2147483648 | bytes 8388608 | tf_op jit(solution)/shard_map/pallas_call | solution.py:246
  41.5 0.3 collective-permute-done.6.low_ref
  41.8 0.0 collective-permute-done.7.high_ref
  41.8 1.7 %blocks.1 = f32[8,144,512]{2,1,0:T(8,128)} custom-call(f32[1024,512]{1,0:T(8,128)S(1)} %shard_map.97.mine_ref, f32[512,512]{1,0:T(8,128)S(1)} %collective-permute-done.6.low_ref, f32[640,512]{1,0:T(8,128)S(1)} %collective-permute-done.7.high_ref, f32[128,1024]{1,0:T(8,128)S(1)} %get-tuple-element.44.refs_3_.small_ref), custom_call_target="tpu_custom_call" | custom-call | flops 524288 | bytes 7340032 | tf_op jit(solution)/shard_map/blocks/pallas_call | solution.py:277
  43.5 7.4 %all-to-all-start = ((f32[8,144,512]{2,1,0:T(8,128)}), f32[8,144,512]{2,1,0:T(8,128)S(1)}, u32[]{:S(2)}, u32[]{:S(2)}) async-start(f32[8,144,512]{2,1,0:T(8,128)} %blocks.1), calls=%async_computation | async-start | bytes 4718592 | tf_op jit(solution)/shard_map/all_to_all | solution.py:71
  50.9 4.0 %copy.10 = bf16[1024,1024]{0,1:T(8,128)(2,1)} copy(bf16[1024,1024]{1,0:T(8,128)(2,1)} %w_any.1) | data formatting | bytes 4194304 | tf_op jit(solution)/shard_map/optimization_barrier | solution.py:421
  54.9 9.0 %latent.1 = bf16[2,1024,1024]{2,1,0:T(8,128)(2,1)} custom-call(bf16[1024,1024]{1,0:T(8,128)(2,1)} %bitcast.15, bf16[2,1024,512]{2,1,0:T(8,128)(2,1)} %copy-done.1, bf16[2,1024,512]{2,1,0:T(8,128)(2,1)} %copy-done.2), custom_call_target="tpu_custom_call" | custom-call | flops 4294967296 | bytes 8388608 | tf_op jit(solution)/shard_map/latent/pallas_call | solution.py:370
  63.8 4.7 %all-to-all-done = f32[8,144,512]{2,1,0:T(8,128)S(1)} async-done(((f32[8,144,512]{2,1,0:T(8,128)}), f32[8,144,512]{2,1,0:T(8,128)S(1)}, u32[]{:S(2)}, u32[]{:S(2)}) %all-to-all-start) | async-done | bytes 2359328 | tf_op jit(solution)/shard_map/all_to_all | solution.py:71
  68.6 0.2 reduce_sum.9
  68.9 0.1 bitcast_select_fusion
  69.0 0.1 pad_maximum_fusion
  69.0 13.0 %all_to_all.15.second_ref = f32[8,48,512]{2,1,0:T(8,128)S(1)} all-to-all(f32[8,48,512]{2,1,0:T(8,128)S(1)} %pad_maximum_fusion), channel_id=1, replica_groups={{0,64,12,76,3,67,15,79},{80,16,92,28,83,19,95,31},{4,68,8,72,7,71,11,75..., dimensions={0} | all-to-all | bytes 1572864 | tf_op jit(solution)/shard_map/all_to_all | solution.py:71
  82.0 0.1 gather.1
  82.1 13.5 %all_to_all.16.third_ref = f32[8,32,512]{2,1,0:T(8,128)S(1)} all-to-all(f32[8,32,512]{2,1,0:T(8,128)S(1)} %get-tuple-element.50), channel_id=1, replica_groups={{0,80,4,84,1,81,5,85},{64,16,68,20,65,17,69,21},{12,92,8,88,13,93,9,89}..., dimensions={0} | all-to-all | bytes 1048576 | tf_op jit(solution)/shard_map/all_to_all | solution.py:71
  95.5 2.8 %collective-permute-start.8 = (f32[160,512]{1,0:T(8,128)S(1)}, f32[160,512]{1,0:T(8,128)S(1)}, u32[]{:S(2)}, u32[]{:S(2)}) collective-permute-start(f32[160,512]{1,0:T(8,128)S(1)} %pick.1.done_ref), channel_id=1, source_target_pairs={{0,32},{1,33},{2,34},{3,35},{4,36},{5,37},{6,38},{7,39},{8,40},{9,... | collective-permute-start | bytes 983048 | tf_op jit(solution)/shard_map/ppermute | solution.py:435
  98.4 1.3 %collective-permute-done.8.other_ref = f32[160,512]{1,0:T(8,128)S(1)} collective-permute-done((f32[160,512]{1,0:T(8,128)S(1)}, f32[160,512]{1,0:T(8,128)S(1)}, u32[]{:S(2)}, u32[]{:S(2)}) %collective-permute-start.8) | collective-permute-done | bytes 327712 | tf_op jit(solution)/shard_map/ppermute | solution.py:435
  99.6 0.8 finish.1
  (11 shorter events, 0.1 us)
Async XLA Ops:
  0.6 0.9 copy-start.5
  1.5 0.7 copy-start.8
  2.2 12.1 %copy-start = (bf16[2,1024,1024]{2,1,0:T(8,128)(2,1)S(1)}, bf16[2,1024,1024]{2,1,0:T(8,128)(2,1)}, u32[]{:S(2)}) copy-start(bf16[2,1024,1024]{2,1,0:T(8,128)(2,1)} %refs_2_.5) | copy-start | bytes 12582916
  2.2 12.1 %copy-start.6 = (bf16[80,1024]{1,0:T(8,128)(2,1)S(1)}, bf16[80,1024]{1,0:T(8,128)(2,1)}, u32[]{:S(2)}) copy-start(bf16[80,1024]{1,0:T(8,128)(2,1)} %f_ref.3) | copy-start | bytes 491524
  10.8 9.9 %collective-permute-start.2 = (f32[2,80,512]{2,1,0:T(8,128)S(1)}, f32[2,80,512]{2,1,0:T(8,128)S(1)}, u32[]{:S(2)}, u32[]{:S(2)}) collective-permute-start(f32[2,80,512]{2,1,0:T(8,128)S(1)} %get-tuple-element.32.own_ref), channel_id=1, source_target_pairs={{0,64},{1,65},{2,66},{3,67},{4,68},{5,69},{6,70},{7,71},{8,72},{9,... | collective-permute-start | bytes 983048 | tf_op jit(solution)/shard_map/ppermute | solution.py:398
  13.4 10.4 %collective-permute-start.1 = (f32[2,80,512]{2,1,0:T(8,128)S(1)}, f32[2,80,512]{2,1,0:T(8,128)S(1)}, u32[]{:S(2)}, u32[]{:S(2)}) collective-permute-start(f32[2,80,512]{2,1,0:T(8,128)S(1)} %get-tuple-element.32.own_ref), channel_id=1, source_target_pairs={{0,32},{1,33},{2,34},{3,35},{4,36},{5,37},{6,38},{7,39},{8,40},{9,... | collective-permute-start | bytes 983048 | tf_op jit(solution)/shard_map/ppermute | solution.py:399
  14.3 9.5 %copy-start.3 = (f32[2,1024,512]{2,1,0:T(8,128)S(1)}, f32[2,1024,512]{2,1,0:T(8,128)}, u32[]{:S(2)}) copy-start(f32[2,1024,512]{2,1,0:T(8,128)} %get-tuple-element.35.slope_ref) | copy-start | bytes 12582916
  14.3 9.5 %copy-start.4 = (f32[80,1024]{1,0:T(8,128)S(1)}, f32[80,1024]{1,0:T(8,128)}, u32[]{:S(2)}) copy-start(f32[80,1024]{1,0:T(8,128)} %obs_ref.3) | copy-start | bytes 983044
  14.3 9.5 %copy-start.7 = (f32[1024]{0:T(1024)S(1)}, f32[1024]{0:T(1024)}, u32[]{:S(2)}) copy-start(f32[1024]{0:T(1024)} %param.8) | copy-start | bytes 12292
  20.8 3.0 %collective-permute-start.3 = (f32[2,80,512]{2,1,0:T(8,128)S(1)}, f32[2,80,512]{2,1,0:T(8,128)S(1)}, u32[]{:S(2)}, u32[]{:S(2)}) collective-permute-start(f32[2,80,512]{2,1,0:T(8,128)S(1)} %collective-permute-done.2.b_ref), channel_id=1, source_target_pairs={{0,32},{1,33},{2,34},{3,35},{4,36},{5,37},{6,38},{7,39},{8,40},{9,... | collective-permute-start | bytes 983048 | tf_op jit(solution)/shard_map/ppermute | solution.py:407
  22.0 9.3 %collective-permute-start = (f32[2,80,512]{2,1,0:T(8,128)S(1)}, f32[2,80,512]{2,1,0:T(8,128)S(1)}, u32[]{:S(2)}, u32[]{:S(2)}) collective-permute-start(f32[2,80,512]{2,1,0:T(8,128)S(1)} %get-tuple-element.31.own_ref), channel_id=1, source_target_pairs={{0,64},{1,65},{2,66},{3,67},{4,68},{5,69},{6,70},{7,71},{8,72},{9,... | collective-permute-start | bytes 983048 | tf_op jit(solution)/shard_map/ppermute | solution.py:398
  23.5 8.7 %collective-permute-start.4 = (f32[2,80,512]{2,1,0:T(8,128)S(1)}, f32[2,80,512]{2,1,0:T(8,128)S(1)}, u32[]{:S(2)}, u32[]{:S(2)}) collective-permute-start(f32[2,80,512]{2,1,0:T(8,128)S(1)} %get-tuple-element.31.own_ref), channel_id=1, source_target_pairs={{0,32},{1,33},{2,34},{3,35},{4,36},{5,37},{6,38},{7,39},{8,40},{9,... | collective-permute-start | bytes 983048 | tf_op jit(solution)/shard_map/ppermute | solution.py:399
  26.3 12.9 %copy-start.1 = (bf16[2,1024,512]{2,1,0:T(8,128)(2,1)}, bf16[2,1024,512]{2,1,0:T(8,128)(2,1)S(1)}, u32[]{:S(2)}) copy-start(bf16[2,1024,512]{2,1,0:T(8,128)(2,1)S(1)} %get-tuple-element.38.refs_0_) | copy-start | bytes 6291460
  31.3 2.1 %collective-permute-start.5 = (f32[2,80,512]{2,1,0:T(8,128)S(1)}, f32[2,80,512]{2,1,0:T(8,128)S(1)}, u32[]{:S(2)}, u32[]{:S(2)}) collective-permute-start(f32[2,80,512]{2,1,0:T(8,128)S(1)} %collective-permute-done.b_ref), channel_id=1, source_target_pairs={{0,32},{1,33},{2,34},{3,35},{4,36},{5,37},{6,38},{7,39},{8,40},{9,... | collective-permute-start | bytes 983048 | tf_op jit(solution)/shard_map/ppermute | solution.py:407
  35.9 3.3 %copy-start.2 = (bf16[2,1024,512]{2,1,0:T(8,128)(2,1)}, bf16[2,1024,512]{2,1,0:T(8,128)(2,1)S(1)}, u32[]{:S(2)}) copy-start(bf16[2,1024,512]{2,1,0:T(8,128)(2,1)S(1)} %get-tuple-element.43.refs_1_) | copy-start | bytes 6291460
  37.2 4.6 %collective-permute-start.7 = (f32[640,512]{1,0:T(8,128)S(1)}, f32[640,512]{1,0:T(8,128)S(1)}, u32[]{:S(2)}, u32[]{:S(2)}) collective-permute-start(f32[640,512]{1,0:T(8,128)S(1)} %shard_map.99), channel_id=1, source_target_pairs={{0,32},{1,33},{2,34},{3,35},{4,36},{5,37},{6,38},{7,39},{8,40},{9,... | collective-permute-start | bytes 3932168 | tf_op jit(solution)/shard_map/ppermute | solution.py:418
  39.0 2.9 %collective-permute-start.6 = (f32[512,512]{1,0:T(8,128)S(1)}, f32[512,512]{1,0:T(8,128)S(1)}, u32[]{:S(2)}, u32[]{:S(2)}) collective-permute-start(f32[512,512]{1,0:T(8,128)S(1)} %shard_map.98), channel_id=1, source_target_pairs={{0,32},{1,33},{2,34},{3,35},{4,36},{5,37},{6,38},{7,39},{8,40},{9,... | collective-permute-start | bytes 3145736 | tf_op jit(solution)/shard_map/ppermute | solution.py:416
  43.5 25.0 %all-to-all-start = ((f32[8,144,512]{2,1,0:T(8,128)}), f32[8,144,512]{2,1,0:T(8,128)S(1)}, u32[]{:S(2)}, u32[]{:S(2)}) async-start(f32[8,144,512]{2,1,0:T(8,128)} %blocks.1), calls=%async_computation | async-start | bytes 4718592 | tf_op jit(solution)/shard_map/all_to_all | solution.py:71
  95.5 4.1 %collective-permute-start.8 = (f32[160,512]{1,0:T(8,128)S(1)}, f32[160,512]{1,0:T(8,128)S(1)}, u32[]{:S(2)}, u32[]{:S(2)}) collective-permute-start(f32[160,512]{1,0:T(8,128)S(1)} %pick.1.done_ref), channel_id=1, source_target_pairs={{0,32},{1,33},{2,34},{3,35},{4,36},{5,37},{6,38},{7,39},{8,40},{9,... | collective-permute-start | bytes 983048 | tf_op jit(solution)/shard_map/ppermute | solution.py:435
